TPU v7x, 256 devices: a whole 4x4x8 slice. The times are simulated.
256 devices in a mesh: row: 8 (over x, core), col: 32 (over z, y).
Axes of the slice: x: 4, y: 4, z: 8, core: 2. Of those that a mesh axis runs over, the one named last changes fastest.
Arguments:
- layer_input: bfloat16 [16896, 1024], P('col', 'row'), may hold values from -6 to 6
- w_q: bfloat16 [1024, 1024], P('col', 'row'), may hold values from -0.1875 to 0.1875
- w_k: bfloat16 [1024, 1024], P('col', 'row'), may hold values from -0.1875 to 0.1875
- w_v: bfloat16 [1024, 1024], P('col', 'row'), may hold values from -0.1875 to 0.1875
- w_o: bfloat16 [1024, 1024], P('row', 'col'), may hold values from -0.375 to 0.375
- w_gate: bfloat16 [1024, 4096], P('col', 'row'), may hold values from -0.1875 to 0.1875
- w_up: bfloat16 [1024, 4096], P('col', 'row'), may hold values from -0.1875 to 0.1875
- w_down: bfloat16 [4096, 1024], P('row', 'col'), may hold values from -0.1875 to 0.1875
- norm1: float32 [1024], replicated, may hold values from 0.5 to 1.5
- norm2: float32 [1024], replicated, may hold values from 0.5 to 1.5
- q_gain: float32 [1024], P('row'), may hold values from 0.5 to 1.5
- k_gain: float32 [1024], P('row'), may hold values from 0.5 to 1.5
- bias_same: float32 [16], P('row'), may hold values from -3 to 3
- bias_diff: float32 [16], P('row'), may hold values from -3 to 3
- pre_variate: int32 [32, 512], P('col'), may hold values from 0 to 7, never falling along the last dimension, each value on 1 to 128 neighbouring positions
- pre_keep: int32 [32, 512], P('col'), may hold values 0 or 1
- dec_variate: int32 [512], P('col'), may hold values from 0 to 7
- dec_len: int32 [512], P('col'), may hold values from 1 to 1023, as said below
- dec_table: int32 [512, 8], P('col'), may hold values from 0 to 31
- dec_holder: int32 [512, 1], P('col'), may hold values from 0 to 31; in each aligned block of 16 rows (0 to 15, 16 to 31, ...) at most 2 rows name the same one
- kv_pool: bfloat16 [1024, 2, 128, 1024], P('col', None, None, 'row'), may hold values from -4 to 4
- page_variates: int32 [1024, 128], P('col'), may hold values from 0 to 7
Outputs:
- hidden: bfloat16 [16896, 1024], P('col', 'row')
- prefill_pages: bfloat16 [128, 2, 128, 1024], P('col', None, None, 'row')
- tail_pages: bfloat16 [512, 2, 128, 1024], P('col', None, None, 'row')
Inputs may be any that keep to these rules, and one draw needn't show every extreme that they name: `pre_variate`: each variate's tokens form one run of at most 128 positions. `dec_len`: some request has exactly 1023 cached tokens. `dec_table`: entries past a request's last page are unused; requests may share pages. `dec_holder`: among the 16 requests of one column group at most 2 name the same holder, a bound that some block reaches of them.
All inputs are finite; a program needn't handle non-finite values. No bound on the sum of `pre_keep` on one device may be relied on, other than what follows from the above.
Results may differ from a plain program's by a relative error of at most 0.015.
Values may be sent and summed in bfloat16 or wider, within the bound.
No kernel may reach another device: no remote copies, remote signals or barrier semaphores. Data moves between devices by JAX's collectives and lax.ppermute only.
A program may use at most 128 MiB of HBM per device.

v0:
```python
import jax
import jax.numpy as jnp
from jax import lax
from jax.sharding import PartitionSpec as P

HD = 64


eps = 1e-05


def as_sent(array):
    return jax.tree.map(lambda a: a.astype(jnp.bfloat16) if a.dtype == jnp.float32 else a, array)


def norm_rows(values, gain_row):
    return values * lax.rsqrt(jnp.mean(values * values, axis=-1, keepdims=True) + eps) * gain_row


def rotate(tensor, places):
    half_size = tensor.shape[-1] // 2
    spacing = jnp.arange(half_size).astype(jnp.float32) * (2.0 / tensor.shape[-1])
    angles = places.astype(jnp.float32)[:, None] * jnp.power(10000.0, -spacing)[None, :]
    cosine = jnp.cos(angles)[:, None, :]
    sine_part = jnp.sin(angles)[:, None, :]
    lower_half = tensor[..., :half_size]
    upper_half = tensor[..., half_size:]
    return jnp.concatenate(
        [
            lower_half * cosine - upper_half * sine_part,
            upper_half * cosine + lower_half * sine_part,
        ],
        axis=-1,
    )


def segment_time(variates):
    places = jnp.arange(variates.shape[0])
    run_start = jnp.concatenate([jnp.ones((1,), dtype=jnp.bool_), variates[1:] != variates[:-1]])
    starts = lax.cummax(jnp.where(run_start, places, 0), axis=0)
    return places - starts


def on_device(
    layer_input,
    w_q,
    w_k,
    w_v,
    w_o,
    w_gate,
    w_up,
    w_down,
    norm1,
    norm2,
    q_gain,
    k_gain,
    bias_same,
    bias_diff,
    pre_variate,
    pre_keep,
    dec_variate,
    dec_len,
    dec_table,
    dec_holder,
    kv_pool,
    page_variates,
):
    row_count = layer_input.shape[0]
    local_width = layer_input.shape[1]
    pre_len = pre_variate.shape[1]
    dec_count = dec_len.shape[0]
    heads_here = local_width // HD
    score_scale = HD ** (-0.5)
    page_size = kv_pool.shape[2]
    page_count = dec_table.shape[1]
    gathered_input = lax.all_gather(layer_input, "row", axis=1, tiled=True)
    normed = norm_rows(gathered_input.astype(jnp.float32), norm1).astype(jnp.bfloat16)
    pieces = (
        lax.all_gather(w_q, "col", axis=0, tiled=True),
        lax.all_gather(w_k, "col", axis=0, tiled=True),
        lax.all_gather(w_v, "col", axis=0, tiled=True),
    )
    columns = normed
    queries = jnp.dot(columns, pieces[0], preferred_element_type=jnp.float32)
    keys_proj = jnp.dot(columns, pieces[1], preferred_element_type=jnp.float32)
    values_proj = jnp.dot(columns, pieces[2], preferred_element_type=jnp.float32)
    places = jnp.concatenate([segment_time(pre_variate[0]), dec_len])
    query_rot = rotate(
        norm_rows(queries.reshape(row_count, heads_here, HD), q_gain.reshape(heads_here, HD)),
        places,
    ).astype(jnp.bfloat16)
    key_rot = rotate(
        norm_rows(keys_proj.reshape(row_count, heads_here, HD), k_gain.reshape(heads_here, HD)),
        places,
    ).astype(jnp.bfloat16)
    value_bf = values_proj.astype(jnp.bfloat16).reshape(row_count, heads_here, HD)

    def attend_slot(inputs):
        float_item, int_item = inputs
        new_query = float_item[:local_width].reshape(heads_here, HD)
        new_key = float_item[local_width : 2 * local_width]
        new_value = float_item[2 * local_width :]
        page_rows = int_item[:page_count]
        length = int_item[page_count]
        variate = int_item[page_count + 1]
        gathered = kv_pool[page_rows]
        cached_keys = gathered[:, 0].reshape(page_count * page_size, heads_here, HD)
        cached_vals = gathered[:, 1].reshape(page_count * page_size, heads_here, HD)
        key_variates = page_variates[page_rows].reshape(page_count * page_size)
        scores = (
            jnp.einsum("hd,khd->hk", new_query, cached_keys, preferred_element_type=jnp.float32)
            * score_scale
        )
        scores = scores + jnp.where(
            (key_variates == variate)[None, :], bias_same[:, None], bias_diff[:, None]
        )
        key_heads = new_key.reshape(heads_here, HD)
        value_heads = new_value.reshape(heads_here, HD)
        own_score = (
            jnp.sum(new_query.astype(jnp.float32) * key_heads.astype(jnp.float32), axis=1)
            * score_scale
            + bias_same
        )
        exp_scores = jnp.where(
            (jnp.arange(page_count * page_size) < length)[None, :], jnp.exp(scores), 0.0
        )
        own_exp = jnp.exp(own_score)
        total_weight = jnp.sum(exp_scores, axis=1) + own_exp
        weights_bf = (exp_scores / total_weight[:, None]).astype(jnp.bfloat16)
        own_weight = (own_exp / total_weight).astype(jnp.bfloat16)
        attended = jnp.einsum(
            "hk,khd->hd", weights_bf, cached_vals, preferred_element_type=jnp.float32
        ) + own_weight.astype(jnp.float32)[:, None] * value_heads.astype(jnp.float32)
        tail_slot = page_rows[length // page_size]
        old_page = kv_pool[tail_slot]
        hit_row = (jnp.arange(page_size) == length % page_size)[None, :, None]
        new_rows = jnp.stack([new_key, new_value])[:, None, :]
        return (
            attended.astype(jnp.bfloat16).reshape(local_width),
            jnp.where(hit_row, new_rows, old_page),
        )

    keep_mask = pre_keep[0]
    variates = pre_variate[0]
    block_rows = min(512, pre_len)
    pre_keys = key_rot[:pre_len]
    pre_values = value_bf[:pre_len]
    block_queries = query_rot[0:block_rows]
    scores = (
        jnp.einsum("qhd,khd->hqk", block_queries, pre_keys, preferred_element_type=jnp.float32)
        * score_scale
    )
    same_var = variates[0:block_rows, None] == variates[None, :]
    scores = scores + jnp.where(same_var[None], bias_same[:, None, None], bias_diff[:, None, None])
    allowed = (keep_mask[None, :] == 1) | (
        jnp.arange(0, block_rows)[:, None] == jnp.arange(pre_len)[None, :]
    )
    exp_scores = jnp.where(allowed[None], jnp.exp(scores), 0.0)
    weights_bf = (exp_scores / jnp.sum(exp_scores, axis=2, keepdims=True)).astype(jnp.bfloat16)
    outputs = jnp.einsum(
        "hqk,khd->qhd", weights_bf, pre_values, preferred_element_type=jnp.float32
    ).astype(jnp.bfloat16)
    prefill_out = outputs.reshape(pre_len, local_width)
    peer_count = lax.axis_size("col")
    slot_count = max(2, (dec_count + peer_count - 1) // peer_count)
    holder = dec_holder[:, 0]
    onehot = (holder[:, None] == jnp.arange(peer_count)[None, :]).astype(jnp.int32)
    slot_rank = jnp.sum((jnp.cumsum(onehot, axis=0) - onehot) * onehot, axis=1)
    target = holder * slot_count + slot_rank
    payload = jnp.concatenate(
        [
            query_rot[pre_len:].reshape(dec_count, local_width),
            key_rot[pre_len:].reshape(dec_count, local_width),
            value_bf[pre_len:].reshape(dec_count, local_width),
        ],
        axis=1,
    )
    int_facts = jnp.concatenate([dec_table, dec_len[:, None], dec_variate[:, None]], axis=1)
    send_float = (
        jnp.zeros((peer_count * slot_count, 3 * local_width), jnp.bfloat16).at[target].set(payload)
    )
    send_int = (
        jnp.zeros((peer_count * slot_count, page_count + 2), jnp.int32).at[target].set(int_facts)
    )
    send_float = send_float.reshape(peer_count, slot_count, 3 * local_width)
    send_int = send_int.reshape(peer_count, slot_count, page_count + 2)
    floats = lax.all_to_all(send_float, "col", split_axis=0, concat_axis=0, tiled=True)
    int_part = lax.all_to_all(send_int, "col", split_axis=0, concat_axis=0, tiled=True)
    group_count = floats.shape[0]
    item_count = floats.shape[1]
    flat_floats = floats.reshape(group_count * item_count, floats.shape[2])
    flat_ints = int_part.reshape(group_count * item_count, int_part.shape[2])
    batch_slots = min(16, group_count * item_count)
    slot_out, slot_tail = lax.map(attend_slot, (flat_floats, flat_ints), batch_size=batch_slots)
    slot_out = slot_out.reshape(group_count, item_count, local_width)
    slot_tail = slot_tail.reshape(group_count, item_count, 2, page_size, local_width)
    back_out = lax.all_to_all(
        as_sent(slot_out), "col", split_axis=0, concat_axis=0, tiled=True
    ).astype(slot_out.dtype)
    back_tail = lax.all_to_all(
        as_sent(slot_tail), "col", split_axis=0, concat_axis=0, tiled=True
    ).astype(slot_tail.dtype)
    decode_out = back_out.reshape(peer_count * slot_count, local_width)[target]
    tails = back_tail.reshape(peer_count * slot_count, 2, page_size, local_width)[target]
    decode_out, tail_pages = (decode_out, tails)
    all_attended = jnp.concatenate([prefill_out, decode_out], axis=0)
    partial_out = jnp.dot(
        all_attended,
        lax.all_gather(w_o, "col", axis=1, tiled=True),
        preferred_element_type=jnp.float32,
    )
    share_start = lax.axis_index("row") * local_width
    attn_total = lax.psum(partial_out.astype(jnp.bfloat16), "row").astype(jnp.float32)
    resid_full = gathered_input.astype(jnp.float32) + attn_total
    ffn_input = norm_rows(resid_full, norm2).astype(jnp.bfloat16)
    resid_share = lax.dynamic_slice_in_dim(resid_full, share_start, local_width, 1)
    zero_hidden = jnp.zeros((row_count, w_gate.shape[1]), jnp.float32)
    pieces = (
        lax.all_gather(w_gate, "col", axis=0, tiled=True),
        lax.all_gather(w_up, "col", axis=0, tiled=True),
    )
    columns = lax.slice_in_dim(ffn_input, 0, pieces[0].shape[0], axis=1)
    gate_proj = zero_hidden + jnp.dot(columns, pieces[0], preferred_element_type=jnp.float32)
    up_proj = zero_hidden + jnp.dot(columns, pieces[1], preferred_element_type=jnp.float32)
    hidden_units = (jax.nn.silu(gate_proj) * up_proj).astype(jnp.bfloat16)
    partial_ffn = jnp.dot(
        hidden_units,
        lax.all_gather(w_down, "col", axis=1, tiled=True),
        preferred_element_type=jnp.float32,
    )
    ffn_share = lax.psum_scatter(
        partial_ffn.astype(jnp.bfloat16), "row", scatter_dimension=1, tiled=True
    ).astype(jnp.float32)
    hidden = (resid_share + ffn_share).astype(jnp.bfloat16)
    prefill_pages = jnp.stack(
        [
            key_rot[:pre_len].reshape(pre_len // page_size, page_size, local_width),
            value_bf[:pre_len].reshape(pre_len // page_size, page_size, local_width),
        ],
        axis=1,
    )
    return (hidden, prefill_pages, tail_pages)


def solution(mesh):
    placed = (
        P("col", "row"),
        P("col", "row"),
        P("col", "row"),
        P("col", "row"),
        P("row", "col"),
        P("col", "row"),
        P("col", "row"),
        P("row", "col"),
        P(),
        P(),
        P("row"),
        P("row"),
        P("row"),
        P("row"),
        P("col", None),
        P("col", None),
        P("col"),
        P("col"),
        P("col", None),
        P("col", None),
        P("col", None, None, "row"),
        P("col", None),
    )
    return jax.shard_map(
        on_device,
        mesh=mesh,
        in_specs=placed,
        out_specs=(P("col", "row"), P("col", None, None, "row"), P("col", None, None, "row")),
        check_vma=False,
    )
```

profile of v0, /device:TPU:38, one launch (start us, length us, event | category | flops | bytes accessed | tf_op | source)
XLA Modules:
  0.0 771.3 jit_solution(16630199738598560226)
XLA Ops:
  15.8 51.5 %all_gather.27 = bf16[1024,128]{1,0:T(8,128)(2,1)S(1)} all-gather(bf16[32,128]{1,0:T(8,128)(2,1)} %param.26), channel_id=1, replica_groups=mesh['row'=8,'col'=32] {'col'}, dimensions={0}, use_global_device_ids=true | all-gather | bytes 270336 | tf_op jit(solution)/shard_map/all_gather | solution.py:80
  67.4 46.8 %all_gather.26 = bf16[1024,128]{1,0:T(8,128)(2,1)S(1)} all-gather(bf16[32,128]{1,0:T(8,128)(2,1)} %param.25), channel_id=1, replica_groups=mesh['row'=8,'col'=32] {'col'}, dimensions={0}, use_global_device_ids=true | all-gather | bytes 270336 | tf_op jit(solution)/shard_map/all_gather | solution.py:79
  114.2 48.2 %all_gather.25 = bf16[1024,128]{1,0:T(8,128)(2,1)S(1)} all-gather(bf16[32,128]{1,0:T(8,128)(2,1)} %param.27), channel_id=1, replica_groups=mesh['row'=8,'col'=32] {'col'}, dimensions={0}, use_global_device_ids=true | all-gather | bytes 270336 | tf_op jit(solution)/shard_map/all_gather | solution.py:81
  162.4 51.0 %all_gather.28 = bf16[128,1024]{0,1:T(8,128)(2,1)} all-gather(bf16[128,32]{0,1:T(8,128)(2,1)} %param.28), channel_id=1, replica_groups=mesh['row'=8,'col'=32] {'col'}, dimensions={1}, use_global_device_ids=true | all-gather | bytes 270336 | tf_op jit(solution)/shard_map/all_gather | solution.py:209
  222.9 7.4 all-to-all-start.1
  230.3 8.9 %all-to-all-done.1 = bf16[32,2,384]{2,1,0:T(2,128)(2,1)S(1)} async-done(((bf16[32,2,384]{2,1,0:T(2,128)(2,1)}), bf16[32,2,384]{2,1,0:T(2,128)(2,1)S(1)}, u32[]{:S(2)}, u32[]{:S(2)}) %all-to-all-start.1) | async-done | bytes 49184 | tf_op jit(solution)/shard_map/all_to_all | solution.py:187
  252.7 209.5 %while.14 = (s32[]{:T(128)}, bf16[4,16,128]{2,1,0:T(8,128)(2,1)}, bf16[4,16,2,128,128]{4,3,2,1,0:T(8,128)(2,1)}, s32[4,16,10]{2,1,0:T(8,128)S(1)}, bf16[4,16,384...) while((s32[]{:T(128)}, bf16[4,16,128]{2,1,0:T(8,128)(2,1)}, ...), condition=%wide.region_13.14_spmd, body=%wide.region_10.13_spmd.sunk | while | flops 9330754 | bytes 80879120 | solution.py:194
  253.8 6.3 gather_fusion
  266.2 6.7 copy.139
  273.0 7.3 squeeze.36
  283.9 6.7 copy.137
  290.7 7.3 squeeze.35
  318.6 6.7 copy.139
  325.4 7.3 squeeze.36
  336.3 6.7 copy.137
  343.1 7.3 squeeze.35
  358.6 6.3 gather_fusion
  371.0 6.7 copy.139
  377.7 7.3 squeeze.36
  388.7 6.7 copy.137
  395.4 7.3 squeeze.35
  410.9 6.3 gather_fusion
  423.4 6.7 copy.139
  430.1 7.3 squeeze.36
  441.1 6.7 copy.137
  447.8 7.3 squeeze.35
  470.1 9.2 %all-to-all-done.2 = bf16[32,2,128]{2,1,0:T(2,128)(2,1)S(1)} async-done(((bf16[32,2,128]{2,1,0:T(2,128)(2,1)}), bf16[32,2,128]{2,1,0:T(2,128)(2,1)S(1)}, u32[]{:S(2)}, u32[]{:S(2)}) %all-to-all-start.2) | async-done | bytes 16416 | tf_op jit(solution)/shard_map/all_to_all | solution.py:197
  488.4 55.6 %all-reduce.2.cloned.1.call-done = bf16[528,1024]{1,0:T(8,128)(2,1)} async-done(((bf16[528,1024]{1,0:T(8,128)(2,1)}), bf16[528,1024]{1,0:T(8,128)(2,1)}) %all-reduce.2.cloned.1.call-update) | async-done | bytes 1081360 | tf_op jit(solution)/shard_map/psum | solution.py:213
  545.7 21.7 %all-gather.7.cloned.1.call-done = bf16[1024,512]{1,0:T(8,128)(2,1)} async-done(((bf16[32,512]{1,0:T(8,128)(2,1)}), bf16[1024,512]{1,0:T(8,128)(2,1)}) %all-gather.7.cloned.1.call-update) | async-done | bytes 1048592 | tf_op jit(solution)/shard_map/all_gather | solution.py:219
  570.7 73.5 %all-gather.11.cloned.1.call-done = bf16[512,1024]{0,1:T(8,128)(2,1)} async-done(((bf16[512,32]{0,1:T(8,128)(2,1)}), bf16[512,1024]{0,1:T(8,128)(2,1)}) %all-gather.11.cloned.1.call-update) | async-done | bytes 1048592 | tf_op jit(solution)/shard_map/all_gather | solution.py:228
  644.2 76.8 %all-gather.9.cloned.1.call-done = bf16[1024,512]{1,0:T(8,128)(2,1)} async-done(((bf16[32,512]{1,0:T(8,128)(2,1)}), bf16[1024,512]{1,0:T(8,128)(2,1)}) %all-gather.9.cloned.1.call-update) | async-done | bytes 1048592 | tf_op jit(solution)/shard_map/all_gather | solution.py:220
  729.0 29.3 %reduce-scatter.4.cloned.1.call-done = bf16[128,528]{1,0:T(8,128)(2,1)} async-done(((bf16[1024,528]{1,0:T(8,128)(2,1)}), bf16[128,528]{1,0:T(8,128)(2,1)}) %reduce-scatter.4.cloned.1.call-update) | async-done | bytes 135184
  (241 shorter events, 143.8 us)
Async XLA Ops:
  8.0 210.1 %copy-start.7 = (f32[1024]{0:T(1024)S(1)}, f32[1024]{0:T(1024)}, u32[]{:S(2)}) copy-start(f32[1024]{0:T(1024)} %param.32) | copy-start | bytes 12292
  8.0 208.4 %all-gather.5.cloned.1.call-start = ((), (), s32[]{:S(2)}) async-start(), calls=%async_computation.5 | async-start | bytes 1216512 | tf_op jit(solution)/shard_map/all_gather | solution.py:76
  216.4 3.5 copy-start.2
  220.8 23.2 %copy-start.5 = (f32[2]{0:T(128)S(1)}, f32[2]{0:T(128)}, u32[]{:S(2)}) copy-start(f32[2]{0:T(128)} %param.36) | copy-start | bytes 28
  220.8 23.2 %copy-start.6 = (f32[2]{0:T(128)S(1)}, f32[2]{0:T(128)}, u32[]{:S(2)}) copy-start(f32[2]{0:T(128)} %param.37) | copy-start | bytes 28
  222.9 16.3 %all-to-all-start.1 = ((bf16[32,2,384]{2,1,0:T(2,128)(2,1)}), bf16[32,2,384]{2,1,0:T(2,128)(2,1)S(1)}, u32[]{:S(2)}, u32[]{:S(2)}) async-start(bf16[32,2,384]{2,1,0:T(2,128)(2,1)} %reshape.400), calls=%async_computation.1 | async-start | bytes 98304 | tf_op jit(solution)/shard_map/all_to_all | solution.py:187
  239.2 13.5 %all-to-all-start = ((s32[32,2,10]{2,1,0:T(2,128)}), s32[32,2,10]{2,1,0:T(2,128)S(1)}, u32[]{:S(2)}, u32[]{:S(2)}) async-start(s32[32,2,10]{2,1,0:T(2,128)} %bitcast.30), calls=%async_computation | async-start | bytes 65536 | tf_op jit(solution)/shard_map/all_to_all | solution.py:188
  244.0 8.7 %copy-start = (bf16[32,2,128,128]{3,2,1,0:T(8,128)(2,1)S(1)}, bf16[32,2,128,128]{3,2,1,0:T(8,128)(2,1)}, u32[]{:S(2)}) copy-start(bf16[32,2,128,128]{3,2,1,0:T(8,128)(2,1)} %param.44) | copy-start | bytes 6291460
  244.0 8.7 %copy-start.1 = (s32[32,128]{1,0:T(8,128)S(1)}, s32[32,128]{1,0:T(8,128)}, u32[]{:S(2)}) copy-start(s32[32,128]{1,0:T(8,128)} %param.45) | copy-start | bytes 49156
  462.3 17.1 %all-to-all-start.2 = ((bf16[32,2,128]{2,1,0:T(2,128)(2,1)}), bf16[32,2,128]{2,1,0:T(2,128)(2,1)S(1)}, u32[]{:S(2)}, u32[]{:S(2)}) async-start(bf16[32,2,128]{2,1,0:T(2,128)(2,1)} %bitcast.34), calls=%async_computation.2 | async-start | bytes 32768 | tf_op jit(solution)/shard_map/all_to_all | solution.py:197
  467.3 76.7 %all-reduce.2.cloned.1.call-start = ((), (), s32[]{:S(2)}) async-start(), calls=%async_computation.6 | async-start | bytes 2162688 | tf_op jit(solution)/shard_map/psum | solution.py:213
  467.3 12.7 %copy-start.4 = (bf16[128,1024]{0,1:T(8,128)(2,1)S(1)}, bf16[128,1024]{0,1:T(8,128)(2,1)}, u32[]{:S(2)}) copy-start(bf16[128,1024]{0,1:T(8,128)(2,1)} %all_gather.28) | copy-start | bytes 786436
  481.6 85.9 %all-gather.7.cloned.1.call-start = ((), (), s32[]{:S(2)}) async-start(), calls=%async_computation.7 | async-start | bytes 1081344 | tf_op jit(solution)/shard_map/all_gather | solution.py:219
  482.1 61.9 %copy-start.3 = (bf16[528,1024]{1,0:T(8,128)(2,1)S(1)}, bf16[528,1024]{1,0:T(8,128)(2,1)}, u32[]{:S(2)}) copy-start(bf16[528,1024]{1,0:T(8,128)(2,1)} %all-gather.5.cloned.1.call-done) | copy-start | bytes 3244036
  482.1 278.0 %all-to-all-start.3 = ((bf16[32,2,2,128,128]{4,3,2,1,0:T(8,128)(2,1)}), bf16[32,2,2,128,128]{4,3,2,1,0:T(8,128)(2,1)}, u32[]{:S(2)}, u32[]{:S(2)}) async-start(bf16[32,2,2,128,128]{4,3,2,1,0:T(8,128)(2,1)} %bitcast.142), calls=%async_computation.3 | async-start | bytes 8388608 | tf_op jit(solution)/shard_map/all_to_all | solution.py:200
  486.9 157.3 %all-gather.11.cloned.1.call-start = ((), (), s32[]{:S(2)}) async-start(), calls=%async_computation.9 | async-start | bytes 1081344 | tf_op jit(solution)/shard_map/all_gather | solution.py:228
  487.5 233.5 %all-gather.9.cloned.1.call-start = ((), (), s32[]{:S(2)}) async-start(), calls=%async_computation.8 | async-start | bytes 1081344 | tf_op jit(solution)/shard_map/all_gather | solution.py:220
  488.1 79.3 %copy-start.8 = (f32[1024]{0:T(1024)S(1)}, f32[1024]{0:T(1024)}, u32[]{:S(2)}) copy-start(f32[1024]{0:T(1024)} %param.33) | copy-start | bytes 12292
  488.1 270.2 %reduce-scatter.4.cloned.1.call-start = ((), (), s32[]{:S(2)}) async-start(), calls=%async_computation.10 | async-start | bytes 1474560
Sparse Core Ops, SparseCore 0:
  10.7 27.8 all-gather.4
  481.7 62.2 all-reduce.1
  728.2 30.0 reduce-scatter.3
Sparse Core Ops, SparseCore 1:
  484.9 82.4 all-gather.6
  570.2 74.0 all-gather.10
  647.0 74.0 all-gather.8
where the time goes:
time: 778 us; the launch traced here: 771 us
  waiting for transfers between devices  283 us (36%)
  blocking collectives  198 us (25%)
  local copies, waits for them, and re-layouts  189 us (24%)
  matrix products  42.3 us (5%)
  starting transfers between devices  22.5 us (3%)
  other arithmetic  21.1 us (3%)
  between operations  15.7 us (2%)
    all_gather x1, waiting for transfers between devices, on_device(): lax.all_gather(w_up, 'col', axis=0, tiled=True)  76.8 us
    all_gather x1, waiting for transfers between devices, on_device(): lax.all_gather(w_down, 'col', axis=1, tiled=True)  73.5 us
    psum x1, waiting for transfers between devices, on_device(): lax.psum(partial_out.astype(jnp.bfloat16), 'row').astype(jnp.float32)  55.6 us
    while x8, local copies, waits for them, and re-layouts  53.9 us
    all_gather x1, blocking collectives, on_device(): lax.all_gather(w_k, 'col', axis=0, tiled=True)  51.5 us
    all_gather x1, blocking collectives, on_device(): lax.all_gather(w_o, 'col', axis=1, tiled=True)  51 us
    all_gather x1, blocking collectives, on_device(): lax.all_gather(w_v, 'col', axis=0, tiled=True)  48.2 us
    all_gather x1, blocking collectives, on_device(): lax.all_gather(w_q, 'col', axis=0, tiled=True)  46.8 us
  transfers between devices with their start and end apart: 10, of which 8 were waited for; matrix products, arithmetic and copies ran while one was open for 4% of the time, Pallas kernels for 0%

commit v1 on v0

v1 whole, which is shorter than its diff:
```python
import functools

import jax
import jax.numpy as jnp
import numpy as np
from jax import lax
from jax.experimental import pallas as pl
from jax.experimental.pallas import tpu as pltpu
from jax.sharding import PartitionSpec as P

HD = 64
EPS = 1e-05
BF = jnp.bfloat16
F32 = jnp.float32


def dot_nt(a, b):
    return lax.dot_general(a, b, (((1,), (1,)), ((), ())), preferred_element_type=F32)


def whole(shape):
    zeros = (0,) * len(shape)
    return pl.BlockSpec(shape, lambda *_: zeros)


def in_order(me_ref, same_ref, other_ref):
    x, core = me_ref[0], me_ref[1]
    chips = same_ref.shape[0]
    parts = []
    for j in range(2 * chips):
        away = lax.rem(x - j // 2 + chips, chips)
        parts.append(jnp.where(core == j % 2, same_ref[away].astype(F32), other_ref[away].astype(F32)))
    return jnp.concatenate(parts, axis=1)


def norm_rotate(t, gain, cos, sin):
    lane = lax.broadcasted_iota(jnp.int32, t.shape, 1)
    first_head = lane < HD
    lower = (lane % HD) < (HD // 2)
    sq = t * t
    s0 = jnp.sum(jnp.where(first_head, sq, 0.0), axis=-1, keepdims=True)
    s1 = jnp.sum(jnp.where(first_head, 0.0, sq), axis=-1, keepdims=True)
    r = jnp.where(first_head, lax.rsqrt(s0 * (1.0 / HD) + EPS), lax.rsqrt(s1 * (1.0 / HD) + EPS))
    t = t * r * gain
    partner = jnp.where(
        lower, pltpu.roll(t, 128 - HD // 2, axis=1), pltpu.roll(t, HD // 2, axis=1)
    )
    return t * cos + partner * sin


def norm_features(x, gain):
    scale = lax.rsqrt(jnp.mean(x * x, axis=-1, keepdims=True) + EPS)
    return (x * scale * gain).astype(BF)


def pack_kernel(table_ref, len_ref, var_ref, holder_ref, x_ref, w_ref, out_ref):
    peers = out_ref.shape[0]
    share = w_ref.shape[0]
    count, entries = table_ref.shape
    w = w_ref[...]
    for c in range(peers):
        out_ref[c, 0:share, :] = w
        out_ref[c, share : share + 8, :] = jnp.zeros((8, 128), BF)
    lane = lax.broadcasted_iota(jnp.int32, (8, 128), 1)
    sub = lax.broadcasted_iota(jnp.int32, (8, 128), 0)
    for r in range(count):
        holder = holder_ref[r, 0]
        rank = jnp.int32(0)
        for p in range(r):
            rank = rank + (holder_ref[p, 0] == holder).astype(jnp.int32)
        length = len_ref[r]
        facts = [table_ref[r, p] for p in range(entries)]
        facts += [length // 128, length % 128, var_ref[r]]
        vec = jnp.zeros((8, 128), jnp.int32)
        for j, fact in enumerate(facts):
            vec = jnp.where(lane == j, fact, vec)
        x = jnp.broadcast_to(x_ref[r : r + 1, :].astype(F32), (8, 128))
        old = out_ref[holder, share : share + 8, :].astype(F32)
        new = jnp.where(sub == rank, vec.astype(F32), jnp.where(sub == rank + 2, x, old))
        out_ref[holder, share : share + 8, :] = new.astype(BF)


def pack_call(table, length, variate, holder, x, w, peers):
    count = length.shape[0]
    smem = pl.BlockSpec(memory_space=pltpu.SMEM)
    shape = (peers, w.shape[0] + 8, 128)
    last = x.shape[0] // count - 1
    return pl.pallas_call(
        pack_kernel,
        grid=(1,),
        in_specs=[
            smem,
            smem,
            smem,
            smem,
            pl.BlockSpec((count, 128), lambda i: (last, 0)),
            whole(w.shape),
        ],
        out_specs=whole(shape),
        out_shape=jax.ShapeDtypeStruct(shape, BF),
        cost_estimate=pl.CostEstimate(flops=0, bytes_accessed=1024 * 1024, transcendentals=0),
        name="pack",
    )(table, length, variate, holder, x, w)


def qkv_kernel(
    me_ref, xa_ref, xb_ref, norm_ref, wq_ref, wk_ref, wv_ref, cos_ref, sin_ref, qg_ref, kg_ref, out_ref
):
    normed = norm_features(in_order(me_ref, xa_ref, xb_ref), norm_ref[...])
    share = wq_ref.shape[1] - 8
    wq = wq_ref[:, 0:share, :].reshape(-1, 128)
    w = jnp.concatenate([wq, wk_ref[...], wv_ref[...]], axis=1)
    proj = jnp.dot(normed, w, preferred_element_type=F32)
    cos = cos_ref[...]
    sin = sin_ref[...]
    out_ref[:, 0:128] = norm_rotate(proj[:, 0:128], qg_ref[...], cos, sin).astype(BF)
    out_ref[:, 128:256] = norm_rotate(proj[:, 128:256], kg_ref[...], cos, sin).astype(BF)
    out_ref[:, 256:384] = proj[:, 256:384].astype(BF)


def qkv_call(me, xa, xb, norm1, got, big, col_block, cos, sin, qg, kg):
    chips, rows, _ = xa.shape
    width = norm1.shape[1]
    step = rows // 3
    row_spec = lambda cols: pl.BlockSpec((step, cols), lambda i: (i, 0))
    x_spec = pl.BlockSpec((chips, step, 128), lambda i: (0, i, 0))
    return pl.pallas_call(
        qkv_kernel,
        grid=(3,),
        in_specs=[
            pl.BlockSpec(memory_space=pltpu.SMEM),
            x_spec,
            x_spec,
            whole((1, width)),
            whole(got.shape),
            pl.BlockSpec((width, 128), lambda i: (0, col_block)),
            pl.BlockSpec((width, 128), lambda i: (0, col_block + 1)),
            row_spec(128),
            row_spec(128),
            whole((1, 128)),
            whole((1, 128)),
        ],
        out_specs=row_spec(384),
        out_shape=jax.ShapeDtypeStruct((rows, 384), BF),
        cost_estimate=pl.CostEstimate(
            flops=2 * rows * width * 384, bytes_accessed=4 * 1024 * 1024, transcendentals=0
        ),
        name="qkv",
    )(me, xa, xb, norm1, got, big, big, cos, sin, qg, kg)


def prefill_kernel(
    qkv_ref, vcol_ref, vrow_ref, keep_ref, bsame_ref, bdiff_ref, out_ref, pages_ref
):
    length = out_ref.shape[0]
    block = 128
    keys = qkv_ref[0:length, 128:256]
    values = qkv_ref[0:length, 256:384]
    for p in range(length // 128):
        pages_ref[p, 0] = qkv_ref[p * 128 : (p + 1) * 128, 128:256]
        pages_ref[p, 1] = qkv_ref[p * 128 : (p + 1) * 128, 256:384]
    lane = lax.broadcasted_iota(jnp.int32, (block, 128), 1)
    first_head = lane < HD
    col = lax.broadcasted_iota(jnp.int32, (block, length), 1)
    row = lax.broadcasted_iota(jnp.int32, (block, length), 0)
    keep = keep_ref[...] == 1
    for b in range(length // block):
        q = qkv_ref[b * block : (b + 1) * block, 0:128]
        same = vcol_ref[b * block : (b + 1) * block, :] == vrow_ref[...]
        allowed = keep | (col == row + b * block)
        outs = []
        for h in range(2):
            qh = jnp.where(first_head if h == 0 else ~first_head, q, jnp.zeros_like(q))
            s = dot_nt(qh, keys) * (HD**-0.5)
            s = s + jnp.where(same, bsame_ref[h], bdiff_ref[h])
            e = jnp.where(allowed, jnp.exp(s), 0.0)
            total = jnp.sum(e, axis=1, keepdims=True)
            w = (e * (1.0 / total)).astype(BF)
            outs.append(jnp.dot(w, values, preferred_element_type=F32))
        out_ref[b * block : (b + 1) * block, :] = jnp.where(first_head, outs[0], outs[1]).astype(BF)


def prefill_call(qkv, vcol, vrow, keep, bsame, bdiff, length, page):
    smem = pl.BlockSpec(memory_space=pltpu.SMEM)
    return pl.pallas_call(
        prefill_kernel,
        grid=(1,),
        in_specs=[
            whole(qkv.shape),
            whole((length, 1)),
            whole((1, length)),
            whole((1, length)),
            smem,
            smem,
        ],
        out_specs=[whole((length, 128)), whole((length // page, 2, page, 128))],
        out_shape=[
            jax.ShapeDtypeStruct((length, 128), BF),
            jax.ShapeDtypeStruct((length // page, 2, page, 128), BF),
        ],
        cost_estimate=pl.CostEstimate(
            flops=8 * length * length * 128,
            bytes_accessed=8 * length * 128 * 2,
            transcendentals=2 * length * length,
        ),
        name="prefill",
    )(qkv, vcol, vrow, keep, bsame, bdiff)


def decode_kernel(
    me_ref,
    xa_ref,
    xb_ref,
    norm_ref,
    w_ref,
    cos_ref,
    sin_ref,
    qg_ref,
    ints_ref,
    bsame_ref,
    bdiff_ref,
    pool_ref,
    pv_ref,
    out_ref,
):
    slots = ints_ref.shape[0]
    pages = pool_ref.shape[0]
    lane = lax.broadcasted_iota(jnp.int32, (slots, 128), 1)
    first_head = lane < HD
    normed = norm_features(in_order(me_ref, xa_ref, xb_ref), norm_ref[...])
    wq = w_ref[:, 0 : w_ref.shape[1] - 8, :].reshape(-1, 128)
    q = jnp.dot(normed, wq, preferred_element_type=F32)
    q = norm_rotate(q, qg_ref[...], cos_ref[...], sin_ref[...]).astype(BF)
    zero = jnp.zeros_like(q)
    q2 = jnp.concatenate([jnp.where(first_head, q, zero), jnp.where(first_head, zero, q)], axis=0)
    rows = lax.broadcasted_iota(jnp.int32, (2 * slots, 1), 0)
    bsame = jnp.where(rows < slots, bsame_ref[0], bsame_ref[1])
    bdiff = jnp.where(rows < slots, bdiff_ref[0], bdiff_ref[1])
    ints = jnp.concatenate([ints_ref[...], ints_ref[...]], axis=0)
    entries = ints.shape[1] // 2
    last = ints[:, entries : entries + 1]
    rem = ints[:, entries + 1 : entries + 2]
    var = ints[:, entries + 2 : entries + 3]
    tok = lax.broadcasted_iota(jnp.int32, (2 * slots, 128), 1)
    in_part = (tok < rem).astype(F32)
    full = jnp.zeros((2 * slots, 128), F32)
    part = jnp.zeros((2 * slots, 128), F32)
    for p in range(entries):
        hit = (ints[:, p : p + 1] == tok).astype(F32)
        full = full + jnp.where(p < last, hit, 0.0)
        part = part + jnp.where(p == last, hit, 0.0)
    acc = jnp.zeros((2 * slots, 128), F32)
    sums = jnp.zeros((2 * slots, 128), F32)
    for g in range(pages):
        s = dot_nt(q2, pool_ref[g, 0]) * (HD**-0.5)
        s = s + jnp.where(pv_ref[g : g + 1, :] == var, bsame, bdiff)
        count = full[:, g : g + 1] + part[:, g : g + 1] * in_part
        e = jnp.exp(s) * count
        sums = sums + e
        acc = acc + jnp.dot(e.astype(BF), pool_ref[g, 1], preferred_element_type=F32)
    total = jnp.sum(sums, axis=1, keepdims=True)
    o = acc / jnp.where(total > 0.0, total, 1.0)
    out_ref[:, 0:128] = jnp.where(first_head, o[0:slots], o[slots:]).astype(BF)
    high = total.astype(BF).astype(F32)
    low = total - high
    out_ref[:, 128:256] = jnp.where(
        lane < 2,
        jnp.where(lane == 0, high[0:slots], high[slots:]),
        jnp.where(lane == 2, low[0:slots], low[slots:]),
    ).astype(BF)


def decode_call(me, xa, xb, norm1, got, cos, sin, qg, ints, bsame, bdiff, pool, pv):
    slots = ints.shape[0]
    smem = pl.BlockSpec(memory_space=pltpu.SMEM)
    args = (me, xa, xb, norm1, got, cos, sin, qg, ints, bsame, bdiff, pool, pv)
    return pl.pallas_call(
        decode_kernel,
        grid=(1,),
        in_specs=[smem if i in (0, 9, 10) else whole(a.shape) for i, a in enumerate(args)],
        out_specs=whole((slots, 256)),
        out_shape=jax.ShapeDtypeStruct((slots, 256), BF),
        cost_estimate=pl.CostEstimate(
            flops=4 * 128 * 128 * 4096, bytes_accessed=3 * 1024 * 1024, transcendentals=128 * 4096
        ),
        name="decode",
    )(*args)


def out_proj_kernel(
    me_ref, bsame_ref, pre_ref, new_ref, back_ref, pick_ref, w_ref, own_ref, other_ref
):
    x, core = me_ref[0], me_ref[1]
    length = pre_ref.shape[0]
    chips = own_ref.shape[0]
    pre = pre_ref[...]
    first_head = lax.broadcasted_iota(jnp.int32, (new_ref.shape[0], 128), 1) < HD
    got = jnp.dot(pick_ref[...], back_ref[...], preferred_element_type=F32)
    total = jnp.where(
        first_head, got[:, 128:129] + got[:, 130:131], got[:, 129:130] + got[:, 131:132]
    )
    qk = new_ref[:, 0:128].astype(F32) * new_ref[:, 128:256].astype(F32)
    s0 = jnp.sum(jnp.where(first_head, qk, 0.0), axis=1, keepdims=True)
    s1 = jnp.sum(jnp.where(first_head, 0.0, qk), axis=1, keepdims=True)
    own = jnp.where(
        first_head,
        jnp.exp(s0 * (HD**-0.5) + bsame_ref[0]),
        jnp.exp(s1 * (HD**-0.5) + bsame_ref[1]),
    )
    value = new_ref[:, 256:384].astype(F32)
    dec = ((got[:, 0:128] * total + own * value) / (total + own)).astype(BF)
    for away in range(chips):
        chip = lax.rem(x + away, chips)
        w = w_ref[pl.ds(pl.multiple_of(chip * 256, 256), 256), :]
        for left, start, size in ((pre, 0, length), (dec, length, dec.shape[0])):
            o = dot_nt(left, w).astype(BF)
            own_ref[away, start : start + size, :] = jnp.where(core == 0, o[:, :128], o[:, 128:])
            other_ref[away, start : start + size, :] = jnp.where(core == 0, o[:, 128:], o[:, :128])


def out_proj_call(me, bsame, pre, qkv, back, pick, big, col_block):
    length = pre.shape[0]
    rows = length + pick.shape[0]
    width = big.shape[0]
    chips = width // 256
    half = jax.ShapeDtypeStruct((chips, rows, 128), BF)
    return pl.pallas_call(
        out_proj_kernel,
        grid=(1,),
        in_specs=[
            pl.BlockSpec(memory_space=pltpu.SMEM),
            pl.BlockSpec(memory_space=pltpu.SMEM),
            whole(pre.shape),
            pl.BlockSpec((pick.shape[0], 384), lambda i: (length // pick.shape[0], 0)),
            whole(back.shape),
            whole(pick.shape),
            pl.BlockSpec((width, 128), lambda i: (0, col_block)),
        ],
        out_specs=[whole(half.shape), whole(half.shape)],
        out_shape=[half, half],
        cost_estimate=pl.CostEstimate(
            flops=2 * rows * 128 * width, bytes_accessed=2 * 1024 * 1024, transcendentals=0
        ),
        name="out_proj",
    )(me, bsame, pre, qkv, back, pick, big)


def ffn_kernel(me_ref, ra_ref, rb_ref, norm_ref, gate_ref, up_ref, down_ref, own_ref, other_ref):
    x, core = me_ref[0], me_ref[1]
    chips = ra_ref.shape[0]
    r = in_order(me_ref, ra_ref, rb_ref)
    scale = lax.rsqrt(jnp.mean(r * r, axis=-1, keepdims=True) + EPS)
    normed = (r * scale * norm_ref[...]).astype(BF)
    gate = jnp.dot(normed, gate_ref[...], preferred_element_type=F32)
    up = jnp.dot(normed, up_ref[...], preferred_element_type=F32)
    units = (gate * (1.0 / (1.0 + jnp.exp(-gate))) * up).astype(BF)
    for away in range(chips):
        chip = lax.rem(x + away, chips)
        w = down_ref[pl.ds(pl.multiple_of(chip * 256, 256), 256), :]
        o = dot_nt(units, w).astype(BF)
        own_ref[away] = jnp.where(core == 0, o[:, :128], o[:, 128:])
        other_ref[away] = jnp.where(core == 0, o[:, 128:], o[:, :128])


def ffn_call(me, ra, rb, norm2, big, hidden):
    chips, rows, _ = ra.shape
    width = big.shape[0]
    step = rows // 3
    w_spec = lambda b: pl.BlockSpec((width, hidden), lambda i: (0, b))
    r_spec = pl.BlockSpec((chips, step, 128), lambda i: (0, i, 0))
    half = jax.ShapeDtypeStruct((chips, rows, 128), BF)
    return pl.pallas_call(
        ffn_kernel,
        grid=(3,),
        in_specs=[
            pl.BlockSpec(memory_space=pltpu.SMEM),
            r_spec,
            r_spec,
            whole((1, width)),
            w_spec(0),
            w_spec(1),
            w_spec(2),
        ],
        out_specs=[r_spec, r_spec],
        out_shape=[half, half],
        cost_estimate=pl.CostEstimate(
            flops=6 * rows * width * hidden, bytes_accessed=6 * 1024 * 1024, transcendentals=0
        ),
        compiler_params=pltpu.CompilerParams(vmem_limit_bytes=32 * 1024 * 1024),
        name="ffn",
    )(me, ra, rb, norm2, big, big, big)


def tail_kernel(target_ref, row_ref, new_ref, pages_ref, out_ref, sem):
    count = out_ref.shape[0]
    copies = [
        pltpu.make_async_copy(pages_ref.at[target_ref[r]], out_ref.at[r], sem.at[r])
        for r in range(count)
    ]
    for c in copies:
        c.start()
    for r in range(count):
        copies[r].wait()
        row = row_ref[r]
        start = pl.multiple_of((row // 16) * 16, 16)
        hit = lax.broadcasted_iota(jnp.int32, (16, 128), 0) == row - start
        for i in range(2):
            new = new_ref[r : r + 1, (1 + i) * 128 : (2 + i) * 128].astype(F32)
            old = out_ref[r, i, pl.ds(start, 16), :].astype(F32)
            out_ref[r, i, pl.ds(start, 16), :] = jnp.where(hit, new, old).astype(BF)


def tail_call(target, row, new, pages):
    count = target.shape[0]
    smem = pl.BlockSpec(memory_space=pltpu.SMEM)
    shape = (count,) + pages.shape[1:]
    return pl.pallas_call(
        tail_kernel,
        grid=(1,),
        in_specs=[
            smem,
            smem,
            pl.BlockSpec((count, 384), lambda i: (new.shape[0] // count - 1, 0)),
            pl.BlockSpec(memory_space=pl.ANY),
        ],
        out_specs=whole(shape),
        out_shape=jax.ShapeDtypeStruct(shape, BF),
        scratch_shapes=[pltpu.SemaphoreType.DMA((count,))],
        cost_estimate=pl.CostEstimate(
            flops=0, bytes_accessed=4 * 1024 * 1024, transcendentals=0
        ),
        name="tail",
    )(target, row, new, pages)


def shifted(x, axis, size, stride, step):
    n = lax.axis_size(axis)
    span = size * stride
    pairs = []
    for i in range(n):
        place = (i % span) // stride
        pairs.append((i, i + ((place + step) % size - place) * stride))
    return lax.ppermute(x, axis, pairs)


def row_gather(v, chips):
    parts = [v] + [shifted(v, "row", chips, 2, d) for d in range(1, chips)]
    same = jnp.stack(parts)
    return same, shifted(same, "row", 2, 1, 1)


def row_scatter(own, other):
    chips = own.shape[0]
    total = own.astype(F32) + shifted(other, "row", 2, 1, 1).astype(F32)
    result = total[0]
    for d in range(1, chips):
        result = result + shifted(total[d].astype(BF), "row", chips, 2, d).astype(F32)
    return result


def exchange(x, axis):
    return lax.all_to_all(x, axis, split_axis=0, concat_axis=0, tiled=True)


def on_device(
    layer_input,
    w_q,
    w_k,
    w_v,
    w_o,
    w_gate,
    w_up,
    w_down,
    norm1,
    norm2,
    q_gain,
    k_gain,
    bias_same,
    bias_diff,
    pre_variate,
    pre_keep,
    dec_variate,
    dec_len,
    dec_table,
    dec_holder,
    kv_pool,
    page_variates,
):
    rows, width = layer_input.shape
    pre_len = pre_variate.shape[1]
    dec_count = dec_len.shape[0]
    hidden = w_gate.shape[1]
    page = kv_pool.shape[2]
    page_count = dec_table.shape[1]
    pool_pages = kv_pool.shape[0]
    peers = lax.axis_size("col")
    slots = 2
    chips = lax.axis_size("row") // 2
    row_at = lax.axis_index("row")
    me = jnp.stack([row_at // 2, row_at % 2]).astype(jnp.int32)

    sent = pack_call(dec_table, dec_len, dec_variate, dec_holder, layer_input, w_q, peers)
    got = exchange(sent, "col")
    big = lax.all_gather(
        jnp.concatenate([w_gate, w_up, w_down.T, w_o.T, w_k, w_v], axis=1),
        "col",
        axis=0,
        tiled=True,
    )
    xa, xb = row_gather(layer_input, chips)

    slot_rows = got[:, -8 : 2 * slots - 8]
    got_x = slot_rows[:, slots:].reshape(peers * slots, width)
    sa, sb = row_gather(got_x, chips)
    got_ints = slot_rows[:, :slots, : 2 * page_count].astype(jnp.int32)
    got_ints = got_ints.reshape(peers * slots, 2 * page_count)
    got_last = got_ints[:, page_count]
    entry = jnp.arange(page_count)[None, :]
    tail_slot = jnp.sum(
        jnp.where(entry == got_last[:, None], got_ints[:, :page_count], 0), axis=1
    )
    old_tails = kv_pool[tail_slot].reshape(peers, slots, 2, page, width)

    half = HD // 2
    spacing = (jnp.arange(width) % half).astype(F32) * (2.0 / HD)
    rates = jnp.power(10000.0, -spacing)[None, :]
    sign = jnp.where((jnp.arange(width) % HD) < half, -1.0, 1.0)[None, :]

    def turns(times):
        angles = times.astype(F32)[:, None] * rates
        return jnp.cos(angles), jnp.sin(angles) * sign

    cos_slots, sin_slots = turns(got_last * page + got_ints[:, page_count + 1])
    dec = decode_call(
        me,
        sa,
        sb,
        norm1[None],
        got,
        cos_slots,
        sin_slots,
        q_gain[None],
        got_ints,
        bias_same,
        bias_diff,
        kv_pool,
        page_variates,
    )
    back = exchange(dec.reshape(peers, slots, 2 * width), "col").reshape(
        peers * slots, 2 * width
    )
    old_tails, back = lax.optimization_barrier((old_tails, back))
    tails = exchange(old_tails, "col")

    holder = dec_holder[:, 0]
    earlier = jnp.arange(dec_count)[:, None] > jnp.arange(dec_count)[None, :]
    rank = jnp.sum(((holder[:, None] == holder[None, :]) & earlier).astype(jnp.int32), axis=1)
    target = holder * slots + rank
    pick = (target[:, None] == jnp.arange(peers * slots)[None, :]).astype(BF)
    variates = pre_variate[0]
    starts = jnp.sum((variates[None, :] < variates[:, None]).astype(jnp.int32), axis=1)
    cos, sin = turns(jnp.concatenate([jnp.arange(pre_len) - starts, dec_len]))

    qkv = qkv_call(
        me,
        xa,
        xb,
        norm1[None],
        got,
        big,
        3 * hidden // width + 1,
        cos,
        sin,
        q_gain[None],
        k_gain[None],
    )
    pre_out, prefill_pages = prefill_call(
        qkv,
        pre_variate.reshape(pre_len, 1),
        pre_variate,
        pre_keep,
        bias_same,
        bias_diff,
        pre_len,
        page,
    )
    own, other = out_proj_call(
        me, bias_same, pre_out, qkv, back, pick, big, 3 * hidden // width
    )
    resid = layer_input.astype(F32) + row_scatter(own, other)
    ra, rb = row_gather(resid.astype(BF), chips)
    own, other = ffn_call(me, ra, rb, norm2[None], big, hidden)
    out = (resid + row_scatter(own, other)).astype(BF)
    tail_pages = tail_call(
        target, dec_len % page, qkv, tails.reshape(peers * slots, 2, page, width)
    )
    return (out, prefill_pages, tail_pages)


def solution(mesh):
    placed = (
        P("col", "row"),
        P("col", "row"),
        P("col", "row"),
        P("col", "row"),
        P("row", "col"),
        P("col", "row"),
        P("col", "row"),
        P("row", "col"),
        P(),
        P(),
        P("row"),
        P("row"),
        P("row"),
        P("row"),
        P("col", None),
        P("col", None),
        P("col"),
        P("col"),
        P("col", None),
        P("col", None),
        P("col", None, None, "row"),
        P("col", None),
    )
    return jax.shard_map(
        on_device,
        mesh=mesh,
        in_specs=placed,
        out_specs=(P("col", "row"), P("col", None, None, "row"), P("col", None, None, "row")),
        check_vma=False,
    )
```

time: 778 us -> 196 us (0.25)
  blocking collectives: 198 us -> 0 us
  waiting for transfers between devices: 283 us -> 95.3 us
  local copies, waits for them, and re-layouts: 189 us -> 14.6 us
  matrix products: 42.3 us -> 0 us
  Pallas kernels: 0 us -> 25.9 us
  starting transfers between devices: 22.5 us -> 36.6 us
  other arithmetic: 21.1 us -> 7.91 us
    all_gather x4 -> x0, blocking collectives: 198 us -> none  [the longest x1 51.5 us: on_device(): lax.all_gather(w_k, 'col', axis=0, tiled=True)]
    all_gather x4 -> x1, waiting for transfers between devices: 172 us -> 26.1 us  [on_device(): lax.all_gather(jnp.concatenate([w_gate, w_up, w_down.T, w_o.T, w_k, w_v],...]
    squeeze x12 -> x0, local copies, waits for them, and re-layouts: 58.4 us -> none  [the longest x4 29.2 us: attend_slot(): cached_keys = gathered[:, 0].reshape(page_count * page_size, heads_here, HD)]
    psum x1 -> x0, waiting for transfers between devices: 55.6 us -> none  [on_device(): lax.psum(partial_out.astype(jnp.bfloat16), 'row').astype(jnp.float32)]
    while x8 -> x0, local copies, waits for them, and re-layouts: 53.9 us -> none
    dot_general x16 -> x0, matrix products: 42.3 us -> none  [the longest x4 13.5 us: attend_slot(): jnp.einsum('hk,khd->hd', weights_bf, cached_vals, preferred_element_type=...]
    gather x19 -> x1, local copies, waits for them, and re-layouts: 38 us -> 3.06 us  [on_device(): old_tails = kv_pool[tail_slot].reshape(peers, slots, 2, page, width)]
    unnamed x7 -> x1, waiting for transfers between devices: 31.6 us -> 0.02 us
  transfers between devices with their start and end apart: 10 -> 24, of which waited for: 8 -> 18; matrix products, arithmetic and copies ran while one was open for 4% -> 8% of each run, Pallas kernels for 0% -> 13%
where the time goes in v1:
time: 196 us; the launch traced here: 195 us
  waiting for transfers between devices  95.3 us (49%)
  starting transfers between devices  36.6 us (19%)
  Pallas kernels  25.9 us (13%)
  local copies, waits for them, and re-layouts  14.6 us (7%)
  between operations  14.4 us (7%)
  other arithmetic  7.91 us (4%)
    all_to_all x3, waiting for transfers between devices, exchange(): return lax.all_to_all(x, axis, split_axis=0, concat_axis=0, tiled=True)  38.9 us
    ppermute x20, waiting for transfers between devices, shifted(): return lax.ppermute(x, axis, pairs)  30.3 us
    all_gather x1, waiting for transfers between devices, on_device(): lax.all_gather(jnp.concatenate([w_gate, w_up, w_down.T, w_o.T, w_k, w_v],...  26.1 us
    all_to_all x3, starting transfers between devices, exchange(): return lax.all_to_all(x, axis, split_axis=0, concat_axis=0, tiled=True)  22 us
    ppermute x20, starting transfers between devices, shifted(): return lax.ppermute(x, axis, pairs)  14.6 us
    unnamed x37, local copies, waits for them, and re-layouts  7.7 us
    pallas_call x1, Pallas kernels, decode_call(): pl.pallas_call(decode_kernel, grid=(1,), in_specs=[smem if i in (0, 9, 10...  5.08 us
    pallas_call x1, Pallas kernels, qkv_call(): pl.pallas_call(qkv_kernel, grid=(3,), in_specs=[pl.BlockSpec(memory_space...  4.72 us
  transfers between devices with their start and end apart: 24, of which 18 were waited for; matrix products, arithmetic and copies ran while one was open for 8% of the time, Pallas kernels for 13%

profile of v1, /device:TPU:38, one launch (start us, length us, event | category | flops | bytes accessed | tf_op | source)
XLA Modules:
  0.0 194.7 jit_solution(16762999752533356017)
XLA Ops:
  12.3 1.4 copy.30.table_ref
  15.0 2.0 %pack.1 = bf16[32,40,128]{2,1,0:T(8,128)(2,1)} custom-call(s32[16,8]{1,0:T(8,128)} %copy.30.table_ref, s32[16]{0:T(128)} %len_ref.1, s32[16]{0:T(128)} %var_ref.1, s32[16,1]{1,0:T(8,128)} %copy.31.holder_ref, bf16[528,128]{1,0:T(8,128)(2,1)} %x_ref.1, bf16[32,128]{1,0:T(8,128)(2,1)} %w_ref.1), custom_call_target="tpu_custom_call" | custom-call | bytes 1048576 | tf_op jit(solution)/shard_map/pack/pallas_call | solution.py:88
  16.9 11.4 %all-to-all-start = ((bf16[32,40,128]{2,1,0:T(8,128)(2,1)}), bf16[32,40,128]{2,1,0:T(8,128)(2,1)S(1)}, u32[]{:S(2)}, u32[]{:S(2)}) async-start(bf16[32,40,128]{2,1,0:T(8,128)(2,1)} %pack.1), calls=%async_computation | async-start | bytes 655360 | tf_op jit(solution)/shard_map/all_to_all | solution.py:462
  29.0 14.6 %all-to-all-done.wq_ref.w_ref = bf16[32,40,128]{2,1,0:T(8,128)(2,1)S(1)} async-done(((bf16[32,40,128]{2,1,0:T(8,128)(2,1)}), bf16[32,40,128]{2,1,0:T(8,128)(2,1)S(1)}, u32[]{:S(2)}, u32[]{:S(2)}) %all-to-all-start) | async-done | bytes 327712 | tf_op jit(solution)/shard_map/all_to_all | solution.py:462
  43.9 2.6 %collective-permute-start.5 = (bf16[64,128]{1,0:T(8,128)(2,1)S(1)}, bf16[64,128]{1,0:T(8,128)(2,1)S(1)}, u32[]{:S(2)}, u32[]{:S(2)}) collective-permute-start(bf16[64,128]{1,0:T(8,128)(2,1)S(1)} %bitcast.91), channel_id=1, source_target_pairs={{0,128},{32,160},{64,192},{96,224},{128,0},{160,32},{192,64},{224,... | collective-permute-start | bytes 49160 | tf_op jit(solution)/shard_map/ppermute | solution.py:443
  49.1 2.3 %collective-permute-done.6 = bf16[64,128]{1,0:T(8,128)(2,1)S(1)} collective-permute-done((bf16[64,128]{1,0:T(8,128)(2,1)S(1)}, bf16[64,128]{1,0:T(8,128)(2,1)S(1)}, u32[]{:S(2)}, u32[]{:S(2)}) %collective-permute-start.6) | collective-permute-done | bytes 16416 | tf_op jit(solution)/shard_map/ppermute | solution.py:443
  53.4 5.1 %decode.1 = bf16[64,256]{1,0:T(8,128)(2,1)} custom-call(s32[2]{0:T(128)} %pad_add_fusion.me_ref, bf16[4,64,128]{2,1,0:T(8,128)(2,1)} %copy-done.9, bf16[4,64,128]{2,1,0:T(8,128)(2,1)} %copy-done.11, f32[1,1024]{1,0:T(1,128)} %bitcast.96, bf16[32,40,128]{2,1,0:T(8,128)(2,1)} %copy-done.4, f32[64,128]{1,0:T(8,128)} %get-tuple-element.32.cos_ref, ...), custom_call_target="tpu_custom_call" | custom-call | flops 268435456 | bytes 3145728 | tf_op jit(solution)/shard_map/decode/pallas_call | solution.py:277
  58.5 1.4 reshape.92
  59.9 4.6 %all-to-all-start.1 = ((bf16[32,2,256]{2,1,0:T(2,128)(2,1)}), bf16[32,2,256]{2,1,0:T(2,128)(2,1)S(1)}, u32[]{:S(2)}, u32[]{:S(2)}) async-start(bf16[32,2,256]{2,1,0:T(2,128)(2,1)} %reshape.92), calls=%async_computation.1 | async-start | bytes 65536 | tf_op jit(solution)/shard_map/all_to_all | solution.py:462
  64.6 3.1 %gather_fusion = bf16[64,2,128,128]{3,2,1,0:T(8,128)(2,1)} fusion(bf16[32,2,128,128]{3,2,1,0:T(8,128)(2,1)S(1)} %copy-done.3, s32[1024]{0:T(1024)S(1)} %pad_clamp_fusion), kind=kCustom, calls=%fused_computation | custom fusion | bytes 8388864 | tf_op jit(solution)/shard_map/gather | solution.py:522
  67.6 5.7 %all-to-all-done.1 = bf16[32,2,256]{2,1,0:T(2,128)(2,1)S(1)} async-done(((bf16[32,2,256]{2,1,0:T(2,128)(2,1)}), bf16[32,2,256]{2,1,0:T(2,128)(2,1)S(1)}, u32[]{:S(2)}, u32[]{:S(2)}) %all-to-all-start.1) | async-done | bytes 32800 | tf_op jit(solution)/shard_map/all_to_all | solution.py:462
  73.9 6.0 %all-to-all-start.2 = ((bf16[32,2,2,128,128]{4,3,2,1,0:T(8,128)(2,1)}), bf16[32,2,2,128,128]{4,3,2,1,0:T(8,128)(2,1)}, u32[]{:S(2)}, u32[]{:S(2)}) async-start(bf16[32,2,2,128,128]{4,3,2,1,0:T(8,128)(2,1)} %bitcast.80), calls=%async_computation.2 | async-start | bytes 8388608 | tf_op jit(solution)/shard_map/all_to_all | solution.py:462
  83.4 2.1 %collective-permute-done = bf16[528,128]{1,0:T(8,128)(2,1)S(1)} collective-permute-done((bf16[528,128]{1,0:T(8,128)(2,1)S(1)}, bf16[528,128]{1,0:T(8,128)(2,1)S(1)}, u32[]{:S(2)}, u32[]{:S(2)}) %collective-permute-start) | collective-permute-done | bytes 135200 | tf_op jit(solution)/shard_map/ppermute | solution.py:443
  85.5 2.2 %collective-permute-done.1 = bf16[528,128]{1,0:T(8,128)(2,1)S(1)} collective-permute-done((bf16[528,128]{1,0:T(8,128)(2,1)S(1)}, bf16[528,128]{1,0:T(8,128)(2,1)S(1)}, u32[]{:S(2)}, u32[]{:S(2)}) %collective-permute-start.1) | collective-permute-done | bytes 135200 | tf_op jit(solution)/shard_map/ppermute | solution.py:443
  89.9 1.8 fusion
  91.8 26.1 %all-gather.2.cloned.1.call-done.wk_ref.wv_ref.w_ref.gate_ref.up_ref.down_ref = bf16[1024,1920]{1,0:T(8,128)(2,1)} async-done(((bf16[32,1920]{1,0:T(8,128)(2,1)}), bf16[1024,1920]{1,0:T(8,128)(2,1)}) %all-gather.2.cloned.1.call-update) | async-done | bytes 3932176 | tf_op jit(solution)/shard_map/all_gather | solution.py:504
  117.9 4.7 %qkv.1.qkv_ref.new_ref = bf16[528,384]{1,0:T(8,128)(2,1)} custom-call(s32[2]{0:T(128)} %pad_add_fusion.me_ref, bf16[4,528,128]{2,1,0:T(8,128)(2,1)} %copy-done.6, bf16[4,528,128]{2,1,0:T(8,128)(2,1)} %copy-done.8, f32[1,1024]{1,0:T(1,128)} %bitcast.97, bf16[32,40,128]{2,1,0:T(8,128)(2,1)} %copy-done.4, ...), custom_call_target="tpu_custom_call" | custom-call | flops 415236096 | bytes 4194304 | tf_op jit(solution)/shard_map/qkv/pallas_call | solution.py:127
  122.6 4.2 %prefill.1 = (bf16[512,128]{1,0:T(8,128)(2,1)}, bf16[4,2,128,128]{3,2,1,0:T(8,128)(2,1)}) custom-call(bf16[528,384]{1,0:T(8,128)(2,1)} %qkv.1.qkv_ref.new_ref, s32[512,1]{1,0:T(8,128)} %copy.32.vcol_ref, s32[1,512]{1,0:T(1,128)} %vrow_ref.1, s32[1,512]{1,0:T(1,128)} %keep_ref.1, f32[2]{0:T(128)} %bsame_ref.5, f32[2]{0:T(128)} %bdiff_ref.3), custom_call_target="tpu_custom_call" | custom-call | flops 268435456 | bytes 1048576 | tf_op jit(solution)/shard_map/prefill/pallas_call | solution.py:185
  126.8 2.9 %out_proj.1 = (bf16[4,528,128]{2,1,0:T(8,128)(2,1)}, bf16[4,528,128]{2,1,0:T(8,128)(2,1)}) custom-call(s32[2]{0:T(128)} %pad_add_fusion.me_ref, f32[2]{0:T(128)} %bsame_ref.5, bf16[512,128]{1,0:T(8,128)(2,1)} %get-tuple-element.11.pre_ref, bf16[528,384]{1,0:T(8,128)(2,1)} %qkv.1.qkv_ref.new_ref, bf16[64,256]{1,0:T(8,128)(2,1)} %reshape.93.back_ref, ...), custom_call_target="tpu_custom_call" | custom-call | flops 138412032 | bytes 2097152 | tf_op jit(solution)/shard_map/out_proj/pallas_call | solution.py:327
  129.7 2.1 %collective-permute-done.8 = bf16[4,528,128]{2,1,0:T(8,128)(2,1)S(1)} collective-permute-done((bf16[4,528,128]{2,1,0:T(8,128)(2,1)}, bf16[4,528,128]{2,1,0:T(8,128)(2,1)S(1)}, u32[]{:S(2)}, u32[]{:S(2)}) %collective-permute-start.8) | collective-permute-done | bytes 540704 | tf_op jit(solution)/shard_map/ppermute | solution.py:443
  131.8 1.3 convert_add_fusion.1
  134.8 2.2 %collective-permute-start.9 = (bf16[528,128]{1,0:T(8,128)(2,1)S(1)}, bf16[528,128]{1,0:T(8,128)(2,1)S(1)}, u32[]{:S(2)}, u32[]{:S(2)}) collective-permute-start(bf16[528,128]{1,0:T(8,128)(2,1)S(1)} %get-tuple-element.26), channel_id=1, source_target_pairs={{0,64},{32,96},{64,128},{96,160},{128,192},{160,224},{192,0},{224,... | collective-permute-start | bytes 405512 | tf_op jit(solution)/shard_map/ppermute | solution.py:443
  137.0 4.2 %collective-permute-done.10 = bf16[528,128]{1,0:T(8,128)(2,1)S(1)} collective-permute-done((bf16[528,128]{1,0:T(8,128)(2,1)S(1)}, bf16[528,128]{1,0:T(8,128)(2,1)S(1)}, u32[]{:S(2)}, u32[]{:S(2)}) %collective-permute-start.10) | collective-permute-done | bytes 135200 | tf_op jit(solution)/shard_map/ppermute | solution.py:443
  141.3 2.0 %collective-permute-done.11 = bf16[528,128]{1,0:T(8,128)(2,1)S(1)} collective-permute-done((bf16[528,128]{1,0:T(8,128)(2,1)S(1)}, bf16[528,128]{1,0:T(8,128)(2,1)S(1)}, u32[]{:S(2)}, u32[]{:S(2)}) %collective-permute-start.11) | collective-permute-done | bytes 135200 | tf_op jit(solution)/shard_map/ppermute | solution.py:443
  145.5 4.4 %collective-permute-done.12 = bf16[528,128]{1,0:T(8,128)(2,1)S(1)} collective-permute-done((bf16[528,128]{1,0:T(8,128)(2,1)S(1)}, bf16[528,128]{1,0:T(8,128)(2,1)S(1)}, u32[]{:S(2)}, u32[]{:S(2)}) %collective-permute-start.12) | collective-permute-done | bytes 135200 | tf_op jit(solution)/shard_map/ppermute | solution.py:443
  149.9 2.0 %collective-permute-done.13 = bf16[528,128]{1,0:T(8,128)(2,1)S(1)} collective-permute-done((bf16[528,128]{1,0:T(8,128)(2,1)S(1)}, bf16[528,128]{1,0:T(8,128)(2,1)S(1)}, u32[]{:S(2)}, u32[]{:S(2)}) %collective-permute-start.13) | collective-permute-done | bytes 135200 | tf_op jit(solution)/shard_map/ppermute | solution.py:443
  151.9 1.6 collective-permute-done.14
  153.7 1.9 collective-permute-done.15.rb_ref
  155.6 4.0 %ffn.1 = (bf16[4,528,128]{2,1,0:T(8,128)(2,1)S(1)}, bf16[4,528,128]{2,1,0:T(8,128)(2,1)S(1)}) custom-call(s32[2]{0:T(128)S(1)} %copy-done.1, bf16[4,528,128]{2,1,0:T(8,128)(2,1)S(1)} %pad_maximum_fusion.1.ra_ref, bf16[4,528,128]{2,1,0:T(8,128)(2,1)S(1)} %collective-permute-done.15.rb_ref, f32[1,1024]{1,0:T(1,128)S(1)} %bitcast.79, ...), custom_call_target="tpu_custom_call" | custom-call | flops 1660944384 | bytes 6291456 | tf_op jit(solution)/shard_map/ffn/pallas_call | solution.py:372
  159.8 1.8 collective-permute-done.16
  165.2 18.7 %all-to-all-done.2 = bf16[32,2,2,128,128]{4,3,2,1,0:T(8,128)(2,1)} async-done(((bf16[32,2,2,128,128]{4,3,2,1,0:T(8,128)(2,1)}), bf16[32,2,2,128,128]{4,3,2,1,0:T(8,128)(2,1)}, u32[]{:S(2)}, u32[]{:S(2)}) %all-to-all-start.2) | async-done | bytes 4194336 | tf_op jit(solution)/shard_map/all_to_all | solution.py:462
  183.9 3.1 %tail.1 = bf16[16,2,128,128]{3,2,1,0:T(8,128)(2,1)} custom-call(s32[16]{0:T(128)} %get-tuple-element.36.target_ref, s32[16]{0:T(128)} %get-tuple-element.35.row_ref, bf16[528,384]{1,0:T(8,128)(2,1)} %qkv.1.qkv_ref.new_ref, bf16[64,2,128,128]{3,2,1,0:T(8,128)(2,1)} %bitcast.39.pages_ref), custom_call_target="tpu_custom_call" | custom-call | bytes 4194304 | tf_op jit(solution)/shard_map/tail/pallas_call | solution.py:417
  (94 shorter events, 27.1 us)
Async XLA Ops:
  7.2 110.7 %all-gather.2.cloned.1.call-start = ((), (), s32[]{:S(2)}) async-start(), calls=%async_computation.3 | async-start | bytes 4055040 | tf_op jit(solution)/shard_map/all_gather | solution.py:504
  16.9 26.6 %all-to-all-start = ((bf16[32,40,128]{2,1,0:T(8,128)(2,1)}), bf16[32,40,128]{2,1,0:T(8,128)(2,1)S(1)}, u32[]{:S(2)}, u32[]{:S(2)}) async-start(bf16[32,40,128]{2,1,0:T(8,128)(2,1)} %pack.1), calls=%async_computation | async-start | bytes 655360 | tf_op jit(solution)/shard_map/all_to_all | solution.py:462
  43.5 9.2 %copy-start.4 = (bf16[32,40,128]{2,1,0:T(8,128)(2,1)}, bf16[32,40,128]{2,1,0:T(8,128)(2,1)S(1)}, u32[]{:S(2)}) copy-start(bf16[32,40,128]{2,1,0:T(8,128)(2,1)S(1)} %all-to-all-done.wq_ref.w_ref) | copy-start | bytes 983044
  43.6 4.3 %collective-permute-start.4 = (bf16[64,128]{1,0:T(8,128)(2,1)S(1)}, bf16[64,128]{1,0:T(8,128)(2,1)S(1)}, u32[]{:S(2)}, u32[]{:S(2)}) collective-permute-start(bf16[64,128]{1,0:T(8,128)(2,1)S(1)} %bitcast.90), channel_id=1, source_target_pairs={{0,64},{32,96},{64,128},{96,160},{128,192},{160,224},{192,0},{224,... | collective-permute-start | bytes 49160 | tf_op jit(solution)/shard_map/ppermute | solution.py:443
  43.9 5.2 %collective-permute-start.5 = (bf16[64,128]{1,0:T(8,128)(2,1)S(1)}, bf16[64,128]{1,0:T(8,128)(2,1)S(1)}, u32[]{:S(2)}, u32[]{:S(2)}) collective-permute-start(bf16[64,128]{1,0:T(8,128)(2,1)S(1)} %bitcast.91), channel_id=1, source_target_pairs={{0,128},{32,160},{64,192},{96,224},{128,0},{160,32},{192,64},{224,... | collective-permute-start | bytes 49160 | tf_op jit(solution)/shard_map/ppermute | solution.py:443
  46.5 4.9 %collective-permute-start.6 = (bf16[64,128]{1,0:T(8,128)(2,1)S(1)}, bf16[64,128]{1,0:T(8,128)(2,1)S(1)}, u32[]{:S(2)}, u32[]{:S(2)}) collective-permute-start(bf16[64,128]{1,0:T(8,128)(2,1)S(1)} %bitcast.92), channel_id=1, source_target_pairs={{0,192},{32,224},{64,0},{96,32},{128,64},{160,96},{192,128},{224,1... | collective-permute-start | bytes 49160 | tf_op jit(solution)/shard_map/ppermute | solution.py:443
  51.4 1.3 collective-permute-start.7
  53.4 11.1 %copy-start.3 = (bf16[32,2,128,128]{3,2,1,0:T(8,128)(2,1)S(1)}, bf16[32,2,128,128]{3,2,1,0:T(8,128)(2,1)}, u32[]{:S(2)}) copy-start(bf16[32,2,128,128]{3,2,1,0:T(8,128)(2,1)} %pool_ref.1) | copy-start | bytes 6291460
  59.9 13.4 %all-to-all-start.1 = ((bf16[32,2,256]{2,1,0:T(2,128)(2,1)}), bf16[32,2,256]{2,1,0:T(2,128)(2,1)S(1)}, u32[]{:S(2)}, u32[]{:S(2)}) async-start(bf16[32,2,256]{2,1,0:T(2,128)(2,1)} %reshape.92), calls=%async_computation.1 | async-start | bytes 65536 | tf_op jit(solution)/shard_map/all_to_all | solution.py:462
  73.9 110.0 %all-to-all-start.2 = ((bf16[32,2,2,128,128]{4,3,2,1,0:T(8,128)(2,1)}), bf16[32,2,2,128,128]{4,3,2,1,0:T(8,128)(2,1)}, u32[]{:S(2)}, u32[]{:S(2)}) async-start(bf16[32,2,2,128,128]{4,3,2,1,0:T(8,128)(2,1)} %bitcast.80), calls=%async_computation.2 | async-start | bytes 8388608 | tf_op jit(solution)/shard_map/all_to_all | solution.py:462
  79.9 9.3 %copy-start.13 = (s32[16]{0:T(128)S(1)}, s32[16]{0:T(128)}, u32[]{:S(2)}) copy-start(s32[16]{0:T(128)} %len_ref.1) | copy-start | bytes 196
  79.9 5.6 %collective-permute-start = (bf16[528,128]{1,0:T(8,128)(2,1)S(1)}, bf16[528,128]{1,0:T(8,128)(2,1)S(1)}, u32[]{:S(2)}, u32[]{:S(2)}) collective-permute-start(bf16[528,128]{1,0:T(8,128)(2,1)S(1)} %copy-done.5), channel_id=1, source_target_pairs={{0,64},{32,96},{64,128},{96,160},{128,192},{160,224},{192,0},{224,... | collective-permute-start | bytes 405512 | tf_op jit(solution)/shard_map/ppermute | solution.py:443
  80.7 7.0 %collective-permute-start.1 = (bf16[528,128]{1,0:T(8,128)(2,1)S(1)}, bf16[528,128]{1,0:T(8,128)(2,1)S(1)}, u32[]{:S(2)}, u32[]{:S(2)}) collective-permute-start(bf16[528,128]{1,0:T(8,128)(2,1)S(1)} %copy-done.5), channel_id=1, source_target_pairs={{0,128},{32,160},{64,192},{96,224},{128,0},{160,32},{192,64},{224,... | collective-permute-start | bytes 405512 | tf_op jit(solution)/shard_map/ppermute | solution.py:443
  81.5 7.4 %collective-permute-start.2 = (bf16[528,128]{1,0:T(8,128)(2,1)S(1)}, bf16[528,128]{1,0:T(8,128)(2,1)S(1)}, u32[]{:S(2)}, u32[]{:S(2)}) collective-permute-start(bf16[528,128]{1,0:T(8,128)(2,1)S(1)} %copy-done.5), channel_id=1, source_target_pairs={{0,192},{32,224},{64,0},{96,32},{128,64},{160,96},{192,128},{224,1... | collective-permute-start | bytes 405512 | tf_op jit(solution)/shard_map/ppermute | solution.py:443
  89.0 28.9 %copy-start.6 = (bf16[4,528,128]{2,1,0:T(8,128)(2,1)}, bf16[4,528,128]{2,1,0:T(8,128)(2,1)S(1)}, u32[]{:S(2)}) copy-start(bf16[4,528,128]{2,1,0:T(8,128)(2,1)S(1)} %pad_maximum_fusion.xa_ref) | copy-start | bytes 1622020
  89.0 2.8 %collective-permute-start.3 = (bf16[4,528,128]{2,1,0:T(8,128)(2,1)S(1)}, bf16[4,528,128]{2,1,0:T(8,128)(2,1)S(1)}, u32[]{:S(2)}, u32[]{:S(2)}) collective-permute-start(bf16[4,528,128]{2,1,0:T(8,128)(2,1)S(1)} %pad_maximum_fusion.xa_ref), channel_id=1, source_target_pairs={{0,32},{32,0},{64,96},{96,64},{128,160},{160,128},{192,224},{224,1... | collective-permute-start | bytes 1622024 | tf_op jit(solution)/shard_map/ppermute | solution.py:443
  91.8 26.1 %copy-start.8 = (bf16[4,528,128]{2,1,0:T(8,128)(2,1)}, bf16[4,528,128]{2,1,0:T(8,128)(2,1)S(1)}, u32[]{:S(2)}) copy-start(bf16[4,528,128]{2,1,0:T(8,128)(2,1)S(1)} %collective-permute-done.3.xb_ref) | copy-start | bytes 1622020
  129.7 2.1 %collective-permute-start.8 = (bf16[4,528,128]{2,1,0:T(8,128)(2,1)}, bf16[4,528,128]{2,1,0:T(8,128)(2,1)S(1)}, u32[]{:S(2)}, u32[]{:S(2)}) collective-permute-start(bf16[4,528,128]{2,1,0:T(8,128)(2,1)} %get-tuple-element.14), channel_id=1, source_target_pairs={{0,32},{32,0},{64,96},{96,64},{128,160},{160,128},{192,224},{224,1... | collective-permute-start | bytes 1622024 | tf_op jit(solution)/shard_map/ppermute | solution.py:443
  131.8 23.8 %copy-start = (bf16[1024,1920]{1,0:T(8,128)(2,1)S(1)}, bf16[1024,1920]{1,0:T(8,128)(2,1)}, u32[]{:S(2)}) copy-start(bf16[1024,1920]{1,0:T(8,128)(2,1)} %all-gather.2.cloned.1.call-done.wk_ref.wv_ref.w_ref.gate_ref.up_ref.down_ref) | copy-start | bytes 11796484
  133.2 22.4 %copy-start.1 = (s32[2]{0:T(128)S(1)}, s32[2]{0:T(128)}, u32[]{:S(2)}) copy-start(s32[2]{0:T(128)} %pad_add_fusion.me_ref) | copy-start | bytes 28
  133.2 22.4 %copy-start.2 = (f32[1024]{0:T(1024)S(1)}, f32[1024]{0:T(1024)}, u32[]{:S(2)}) copy-start(f32[1024]{0:T(1024)} %param.31) | copy-start | bytes 12292
  133.2 8.1 %collective-permute-start.10 = (bf16[528,128]{1,0:T(8,128)(2,1)S(1)}, bf16[528,128]{1,0:T(8,128)(2,1)S(1)}, u32[]{:S(2)}, u32[]{:S(2)}) collective-permute-start(bf16[528,128]{1,0:T(8,128)(2,1)S(1)} %get-tuple-element.28), channel_id=1, source_target_pairs={{0,128},{32,160},{64,192},{96,224},{128,0},{160,32},{192,64},{224,... | collective-permute-start | bytes 405512 | tf_op jit(solution)/shard_map/ppermute | solution.py:443
  133.8 9.5 %collective-permute-start.11 = (bf16[528,128]{1,0:T(8,128)(2,1)S(1)}, bf16[528,128]{1,0:T(8,128)(2,1)S(1)}, u32[]{:S(2)}, u32[]{:S(2)}) collective-permute-start(bf16[528,128]{1,0:T(8,128)(2,1)S(1)} %get-tuple-element.27), channel_id=1, source_target_pairs={{0,192},{32,224},{64,0},{96,32},{128,64},{160,96},{192,128},{224,1... | collective-permute-start | bytes 405512 | tf_op jit(solution)/shard_map/ppermute | solution.py:443
  134.8 8.5 %collective-permute-start.9 = (bf16[528,128]{1,0:T(8,128)(2,1)S(1)}, bf16[528,128]{1,0:T(8,128)(2,1)S(1)}, u32[]{:S(2)}, u32[]{:S(2)}) collective-permute-start(bf16[528,128]{1,0:T(8,128)(2,1)S(1)} %get-tuple-element.26), channel_id=1, source_target_pairs={{0,64},{32,96},{64,128},{96,160},{128,192},{160,224},{192,0},{224,... | collective-permute-start | bytes 405512 | tf_op jit(solution)/shard_map/ppermute | solution.py:443
  143.4 6.5 %collective-permute-start.12 = (bf16[528,128]{1,0:T(8,128)(2,1)S(1)}, bf16[528,128]{1,0:T(8,128)(2,1)S(1)}, u32[]{:S(2)}, u32[]{:S(2)}) collective-permute-start(bf16[528,128]{1,0:T(8,128)(2,1)S(1)} %fusion.25), channel_id=1, source_target_pairs={{0,64},{32,96},{64,128},{96,160},{128,192},{160,224},{192,0},{224,... | collective-permute-start | bytes 405512 | tf_op jit(solution)/shard_map/ppermute | solution.py:443
  144.2 7.7 %collective-permute-start.13 = (bf16[528,128]{1,0:T(8,128)(2,1)S(1)}, bf16[528,128]{1,0:T(8,128)(2,1)S(1)}, u32[]{:S(2)}, u32[]{:S(2)}) collective-permute-start(bf16[528,128]{1,0:T(8,128)(2,1)S(1)} %fusion.25), channel_id=1, source_target_pairs={{0,128},{32,160},{64,192},{96,224},{128,0},{160,32},{192,64},{224,... | collective-permute-start | bytes 405512 | tf_op jit(solution)/shard_map/ppermute | solution.py:443
  145.5 7.9 %collective-permute-start.14 = (bf16[528,128]{1,0:T(8,128)(2,1)S(1)}, bf16[528,128]{1,0:T(8,128)(2,1)S(1)}, u32[]{:S(2)}, u32[]{:S(2)}) collective-permute-start(bf16[528,128]{1,0:T(8,128)(2,1)S(1)} %fusion.25), channel_id=1, source_target_pairs={{0,192},{32,224},{64,0},{96,32},{128,64},{160,96},{192,128},{224,1... | collective-permute-start | bytes 405512 | tf_op jit(solution)/shard_map/ppermute | solution.py:443
  153.5 2.0 %collective-permute-start.15 = (bf16[4,528,128]{2,1,0:T(8,128)(2,1)S(1)}, bf16[4,528,128]{2,1,0:T(8,128)(2,1)S(1)}, u32[]{:S(2)}, u32[]{:S(2)}) collective-permute-start(bf16[4,528,128]{2,1,0:T(8,128)(2,1)S(1)} %pad_maximum_fusion.1.ra_ref), channel_id=1, source_target_pairs={{0,32},{32,0},{64,96},{96,64},{128,160},{160,128},{192,224},{224,1... | collective-permute-start | bytes 1622024 | tf_op jit(solution)/shard_map/ppermute | solution.py:443
  159.6 2.0 %collective-permute-start.16 = (bf16[4,528,128]{2,1,0:T(8,128)(2,1)S(1)}, bf16[4,528,128]{2,1,0:T(8,128)(2,1)S(1)}, u32[]{:S(2)}, u32[]{:S(2)}) collective-permute-start(bf16[4,528,128]{2,1,0:T(8,128)(2,1)S(1)} %get-tuple-element.16), channel_id=1, source_target_pairs={{0,32},{32,0},{64,96},{96,64},{128,160},{160,128},{192,224},{224,1... | collective-permute-start | bytes 1622024 | tf_op jit(solution)/shard_map/ppermute | solution.py:443
  161.8 25.2 %collective-permute-start.17 = (bf16[528,128]{1,0:T(8,128)(2,1)S(1)}, bf16[528,128]{1,0:T(8,128)(2,1)S(1)}, u32[]{:S(2)}, u32[]{:S(2)}) collective-permute-start(bf16[528,128]{1,0:T(8,128)(2,1)S(1)} %get-tuple-element.23), channel_id=1, source_target_pairs={{0,64},{32,96},{64,128},{96,160},{128,192},{160,224},{192,0},{224,... | collective-permute-start | bytes 405512 | tf_op jit(solution)/shard_map/ppermute | solution.py:443
  162.9 24.1 %collective-permute-start.18 = (bf16[528,128]{1,0:T(8,128)(2,1)S(1)}, bf16[528,128]{1,0:T(8,128)(2,1)S(1)}, u32[]{:S(2)}, u32[]{:S(2)}) collective-permute-start(bf16[528,128]{1,0:T(8,128)(2,1)S(1)} %get-tuple-element.25), channel_id=1, source_target_pairs={{0,128},{32,160},{64,192},{96,224},{128,0},{160,32},{192,64},{224,... | collective-permute-start | bytes 405512 | tf_op jit(solution)/shard_map/ppermute | solution.py:443
  163.8 23.1 %collective-permute-start.19 = (bf16[528,128]{1,0:T(8,128)(2,1)S(1)}, bf16[528,128]{1,0:T(8,128)(2,1)S(1)}, u32[]{:S(2)}, u32[]{:S(2)}) collective-permute-start(bf16[528,128]{1,0:T(8,128)(2,1)S(1)} %get-tuple-element.24), channel_id=1, source_target_pairs={{0,192},{32,224},{64,0},{96,32},{128,64},{160,96},{192,128},{224,1... | collective-permute-start | bytes 405512 | tf_op jit(solution)/shard_map/ppermute | solution.py:443
  (7 other events, 32.0 us)
Sparse Core Ops, SparseCore 0:
  12.4 105.4 all-gather.1

commit v2 on v1

--- a/solution.py
+++ b/solution.py
@@ -53,10 +53,11 @@
     return (x * scale * gain).astype(BF)
 
 
-def pack_kernel(table_ref, len_ref, var_ref, holder_ref, x_ref, w_ref, out_ref):
+def pack_kernel(table_ref, len_ref, var_ref, holder_ref, x_ref, w_ref, *refs):
+    parts, (out_ref, wide_ref) = refs[:-2], refs[-2:]
     peers = out_ref.shape[0]
     share = w_ref.shape[0]
-    count, entries = table_ref.shape
+    entries, count = table_ref.shape
     w = w_ref[...]
     for c in range(peers):
         out_ref[c, 0:share, :] = w
@@ -64,12 +65,12 @@
     lane = lax.broadcasted_iota(jnp.int32, (8, 128), 1)
     sub = lax.broadcasted_iota(jnp.int32, (8, 128), 0)
     for r in range(count):
-        holder = holder_ref[r, 0]
+        holder = holder_ref[0, r]
         rank = jnp.int32(0)
         for p in range(r):
-            rank = rank + (holder_ref[p, 0] == holder).astype(jnp.int32)
+            rank = rank + (holder_ref[0, p] == holder).astype(jnp.int32)
         length = len_ref[r]
-        facts = [table_ref[r, p] for p in range(entries)]
+        facts = [table_ref[p, r] for p in range(entries)]
         facts += [length // 128, length % 128, var_ref[r]]
         vec = jnp.zeros((8, 128), jnp.int32)
         for j, fact in enumerate(facts):
@@ -78,12 +79,17 @@
         old = out_ref[holder, share : share + 8, :].astype(F32)
         new = jnp.where(sub == rank, vec.astype(F32), jnp.where(sub == rank + 2, x, old))
         out_ref[holder, share : share + 8, :] = new.astype(BF)
-
-
-def pack_call(table, length, variate, holder, x, w, peers):
+    start = 0
+    for part in parts:
+        wide_ref[:, start : start + part.shape[1]] = part[...]
+        start += part.shape[1]
+
+
+def pack_call(table, length, variate, holder, x, w, peers, parts):
     count = length.shape[0]
     smem = pl.BlockSpec(memory_space=pltpu.SMEM)
     shape = (peers, w.shape[0] + 8, 128)
+    wide = (w.shape[0], sum(p.shape[1] for p in parts))
     last = x.shape[0] // count - 1
     return pl.pallas_call(
         pack_kernel,
@@ -95,37 +101,33 @@
             smem,
             pl.BlockSpec((count, 128), lambda i: (last, 0)),
             whole(w.shape),
-        ],
-        out_specs=whole(shape),
-        out_shape=jax.ShapeDtypeStruct(shape, BF),
+        ]
+        + [whole(p.shape) for p in parts],
+        out_specs=[whole(shape), whole(wide)],
+        out_shape=[jax.ShapeDtypeStruct(shape, BF), jax.ShapeDtypeStruct(wide, BF)],
         cost_estimate=pl.CostEstimate(flops=0, bytes_accessed=1024 * 1024, transcendentals=0),
         name="pack",
-    )(table, length, variate, holder, x, w)
-
-
-def qkv_kernel(
-    me_ref, xa_ref, xb_ref, norm_ref, wq_ref, wk_ref, wv_ref, cos_ref, sin_ref, qg_ref, kg_ref, out_ref
+    )(table, length, variate, holder, x, w, *parts)
+
+
+def early_kernel(
+    me_ref, xa_ref, xb_ref, norm_ref, wq_ref, cos_ref, sin_ref, qg_ref, normed_ref, q_ref
 ):
     normed = norm_features(in_order(me_ref, xa_ref, xb_ref), norm_ref[...])
-    share = wq_ref.shape[1] - 8
-    wq = wq_ref[:, 0:share, :].reshape(-1, 128)
-    w = jnp.concatenate([wq, wk_ref[...], wv_ref[...]], axis=1)
-    proj = jnp.dot(normed, w, preferred_element_type=F32)
-    cos = cos_ref[...]
-    sin = sin_ref[...]
-    out_ref[:, 0:128] = norm_rotate(proj[:, 0:128], qg_ref[...], cos, sin).astype(BF)
-    out_ref[:, 128:256] = norm_rotate(proj[:, 128:256], kg_ref[...], cos, sin).astype(BF)
-    out_ref[:, 256:384] = proj[:, 256:384].astype(BF)
-
-
-def qkv_call(me, xa, xb, norm1, got, big, col_block, cos, sin, qg, kg):
+    normed_ref[...] = normed
+    wq = wq_ref[:, 0 : wq_ref.shape[1] - 8, :].reshape(-1, 128)
+    q = jnp.dot(normed, wq, preferred_element_type=F32)
+    q_ref[...] = norm_rotate(q, qg_ref[...], cos_ref[...], sin_ref[...]).astype(BF)
+
+
+def early_call(me, xa, xb, norm1, got, cos, sin, qg):
     chips, rows, _ = xa.shape
     width = norm1.shape[1]
     step = rows // 3
     row_spec = lambda cols: pl.BlockSpec((step, cols), lambda i: (i, 0))
     x_spec = pl.BlockSpec((chips, step, 128), lambda i: (0, i, 0))
     return pl.pallas_call(
-        qkv_kernel,
+        early_kernel,
         grid=(3,),
         in_specs=[
             pl.BlockSpec(memory_space=pltpu.SMEM),
@@ -133,39 +135,80 @@
             x_spec,
             whole((1, width)),
             whole(got.shape),
-            pl.BlockSpec((width, 128), lambda i: (0, col_block)),
-            pl.BlockSpec((width, 128), lambda i: (0, col_block + 1)),
             row_spec(128),
             row_spec(128),
             whole((1, 128)),
-            whole((1, 128)),
         ],
-        out_specs=row_spec(384),
-        out_shape=jax.ShapeDtypeStruct((rows, 384), BF),
+        out_specs=[row_spec(width), row_spec(128)],
+        out_shape=[
+            jax.ShapeDtypeStruct((rows, width), BF),
+            jax.ShapeDtypeStruct((rows, 128), BF),
+        ],
         cost_estimate=pl.CostEstimate(
-            flops=2 * rows * width * 384, bytes_accessed=4 * 1024 * 1024, transcendentals=0
+            flops=2 * rows * width * 128, bytes_accessed=4 * 1024 * 1024, transcendentals=0
         ),
-        name="qkv",
-    )(me, xa, xb, norm1, got, big, big, cos, sin, qg, kg)
-
-
-def prefill_kernel(
-    qkv_ref, vcol_ref, vrow_ref, keep_ref, bsame_ref, bdiff_ref, out_ref, pages_ref
+        name="early",
+    )(me, xa, xb, norm1, got, cos, sin, qg)
+
+
+def attn_kernel(
+    me_ref,
+    bsame_ref,
+    bdiff_ref,
+    normed_ref,
+    q_ref,
+    wk_ref,
+    wv_ref,
+    wo_ref,
+    cos_ref,
+    sin_ref,
+    kg_ref,
+    vcol_ref,
+    vrow_ref,
+    keep_ref,
+    back_ref,
+    pick_ref,
+    picksum_ref,
+    new_ref,
+    pages_ref,
+    own_ref,
+    other_ref,
+    k_ref,
+    v_ref,
 ):
-    length = out_ref.shape[0]
+    x, core = me_ref[0], me_ref[1]
+    length = vcol_ref.shape[0]
+    rows = q_ref.shape[0]
+    chips = own_ref.shape[0]
     block = 128
-    keys = qkv_ref[0:length, 128:256]
-    values = qkv_ref[0:length, 256:384]
-    for p in range(length // 128):
-        pages_ref[p, 0] = qkv_ref[p * 128 : (p + 1) * 128, 128:256]
-        pages_ref[p, 1] = qkv_ref[p * 128 : (p + 1) * 128, 256:384]
+    w = jnp.concatenate([wk_ref[...], wv_ref[...]], axis=1)
+    for start in range(0, rows, block):
+        end = min(start + block, rows)
+        proj = jnp.dot(normed_ref[start:end, :], w, preferred_element_type=F32)
+        k = norm_rotate(proj[:, 0:128], kg_ref[...], cos_ref[start:end, :], sin_ref[start:end, :])
+        k_ref[start:end, :] = k.astype(BF)
+        v_ref[start:end, :] = proj[:, 128:256].astype(BF)
+
+    def put(left, start):
+        size = left.shape[0]
+        for away in range(chips):
+            chip = lax.rem(x + away, chips)
+            w_o = wo_ref[pl.ds(pl.multiple_of(chip * 256, 256), 256), :]
+            o = dot_nt(left, w_o).astype(BF)
+            own_ref[away, start : start + size, :] = jnp.where(core == 0, o[:, :128], o[:, 128:])
+            other_ref[away, start : start + size, :] = jnp.where(core == 0, o[:, 128:], o[:, :128])
+
+    keys = k_ref[0:length, :]
+    values = v_ref[0:length, :]
     lane = lax.broadcasted_iota(jnp.int32, (block, 128), 1)
     first_head = lane < HD
     col = lax.broadcasted_iota(jnp.int32, (block, length), 1)
     row = lax.broadcasted_iota(jnp.int32, (block, length), 0)
     keep = keep_ref[...] == 1
     for b in range(length // block):
-        q = qkv_ref[b * block : (b + 1) * block, 0:128]
+        q = q_ref[b * block : (b + 1) * block, :]
+        pages_ref[b, 0] = k_ref[b * block : (b + 1) * block, :]
+        pages_ref[b, 1] = v_ref[b * block : (b + 1) * block, :]
         same = vcol_ref[b * block : (b + 1) * block, :] == vrow_ref[...]
         allowed = keep | (col == row + b * block)
         outs = []
@@ -175,36 +218,69 @@
             s = s + jnp.where(same, bsame_ref[h], bdiff_ref[h])
             e = jnp.where(allowed, jnp.exp(s), 0.0)
             total = jnp.sum(e, axis=1, keepdims=True)
-            w = (e * (1.0 / total)).astype(BF)
-            outs.append(jnp.dot(w, values, preferred_element_type=F32))
-        out_ref[b * block : (b + 1) * block, :] = jnp.where(first_head, outs[0], outs[1]).astype(BF)
-
-
-def prefill_call(qkv, vcol, vrow, keep, bsame, bdiff, length, page):
+            weights = (e * (1.0 / total)).astype(BF)
+            outs.append(jnp.dot(weights, values, preferred_element_type=F32))
+        put(jnp.where(first_head, outs[0], outs[1]).astype(BF), b * block)
+
+    kd = k_ref[length:rows, :]
+    vd = v_ref[length:rows, :]
+    new_ref[:, 0:128] = kd
+    new_ref[:, 128:256] = vd
+    first_head = first_head[0 : rows - length]
+    got = jnp.dot(pick_ref[...], back_ref[...], preferred_element_type=F32)
+    sums = jnp.dot(picksum_ref[...], back_ref[...], preferred_element_type=F32)
+    total = jnp.where(first_head, sums[:, 0:1] + sums[:, 2:3], sums[:, 1:2] + sums[:, 3:4])
+    qk = q_ref[length:rows, :].astype(F32) * kd.astype(F32)
+    s0 = jnp.sum(jnp.where(first_head, qk, 0.0), axis=1, keepdims=True)
+    s1 = jnp.sum(jnp.where(first_head, 0.0, qk), axis=1, keepdims=True)
+    own = jnp.where(
+        first_head,
+        jnp.exp(s0 * (HD**-0.5) + bsame_ref[0]),
+        jnp.exp(s1 * (HD**-0.5) + bsame_ref[1]),
+    )
+    put(((got * total + own * vd.astype(F32)) / (total + own)).astype(BF), length)
+
+
+def attn_call(
+    me, bsame, bdiff, normed, q, big, col_block, cos, sin, kg, vcol, vrow, keep, back, pick, picksum
+):
+    rows, width = normed.shape
+    length = vcol.shape[0]
+    chips = width // 256
     smem = pl.BlockSpec(memory_space=pltpu.SMEM)
+    w_spec = lambda j: pl.BlockSpec((width, 128), lambda i: (0, col_block + j))
+    half = jax.ShapeDtypeStruct((chips, rows, 128), BF)
+    shapes = [
+        jax.ShapeDtypeStruct((rows - length, 256), BF),
+        jax.ShapeDtypeStruct((length // 128, 2, 128, 128), BF),
+        half,
+        half,
+    ]
+    tail = (cos, sin, kg, vcol, vrow, keep, back, pick, picksum)
     return pl.pallas_call(
-        prefill_kernel,
+        attn_kernel,
         grid=(1,),
         in_specs=[
-            whole(qkv.shape),
-            whole((length, 1)),
-            whole((1, length)),
-            whole((1, length)),
-            smem,
-            smem,
-        ],
-        out_specs=[whole((length, 128)), whole((length // page, 2, page, 128))],
-        out_shape=[
-            jax.ShapeDtypeStruct((length, 128), BF),
-            jax.ShapeDtypeStruct((length // page, 2, page, 128), BF),
-        ],
+            smem,
+            smem,
+            smem,
+            whole(normed.shape),
+            whole(q.shape),
+            w_spec(1),
+            w_spec(2),
+            w_spec(0),
+        ]
+        + [whole(t.shape) for t in tail],
+        out_specs=[whole(t.shape) for t in shapes],
+        out_shape=shapes,
+        scratch_shapes=[pltpu.VMEM((rows, 128), BF), pltpu.VMEM((rows, 128), BF)],
         cost_estimate=pl.CostEstimate(
-            flops=8 * length * length * 128,
-            bytes_accessed=8 * length * 128 * 2,
+            flops=8 * length * length * 128 + 6 * rows * width * 128,
+            bytes_accessed=6 * 1024 * 1024,
             transcendentals=2 * length * length,
         ),
-        name="prefill",
-    )(qkv, vcol, vrow, keep, bsame, bdiff)
+        name="attn",
+    )(me, bsame, bdiff, normed, q, big, big, big, *tail)
 
 
 def decode_kernel(
@@ -260,89 +336,42 @@
         acc = acc + jnp.dot(e.astype(BF), pool_ref[g, 1], preferred_element_type=F32)
     total = jnp.sum(sums, axis=1, keepdims=True)
     o = acc / jnp.where(total > 0.0, total, 1.0)
-    out_ref[:, 0:128] = jnp.where(first_head, o[0:slots], o[slots:]).astype(BF)
+    o = jnp.where(first_head, o[0:slots], o[slots:]).astype(BF)
     high = total.astype(BF).astype(F32)
     low = total - high
-    out_ref[:, 128:256] = jnp.where(
+    sums = jnp.where(
         lane < 2,
         jnp.where(lane == 0, high[0:slots], high[slots:]),
         jnp.where(lane == 2, low[0:slots], low[slots:]),
     ).astype(BF)
+    peers = out_ref.shape[0]
+    each = slots // peers
+    at = lax.broadcasted_iota(jnp.int32, (8 * peers, slots), 0)
+    slot = lax.broadcasted_iota(jnp.int32, (8 * peers, slots), 1)
+    inner = at % 8
+    slot = slot - (at // 8) * each
+    put_o = ((inner == slot) & (slot >= 0) & (slot < each)).astype(BF)
+    put_sums = ((inner == slot + each) & (slot >= 0) & (slot < each)).astype(BF)
+    rows = jnp.dot(put_o, o, preferred_element_type=F32)
+    rows = rows + jnp.dot(put_sums, sums, preferred_element_type=F32)
+    out_ref[...] = rows.reshape(peers, 8, 128).astype(BF)
 
 
 def decode_call(me, xa, xb, norm1, got, cos, sin, qg, ints, bsame, bdiff, pool, pv):
-    slots = ints.shape[0]
+    peers = got.shape[0]
     smem = pl.BlockSpec(memory_space=pltpu.SMEM)
     args = (me, xa, xb, norm1, got, cos, sin, qg, ints, bsame, bdiff, pool, pv)
     return pl.pallas_call(
         decode_kernel,
         grid=(1,),
         in_specs=[smem if i in (0, 9, 10) else whole(a.shape) for i, a in enumerate(args)],
-        out_specs=whole((slots, 256)),
-        out_shape=jax.ShapeDtypeStruct((slots, 256), BF),
+        out_specs=whole((peers, 8, 128)),
+        out_shape=jax.ShapeDtypeStruct((peers, 8, 128), BF),
         cost_estimate=pl.CostEstimate(
             flops=4 * 128 * 128 * 4096, bytes_accessed=3 * 1024 * 1024, transcendentals=128 * 4096
         ),
         name="decode",
     )(*args)
-
-
-def out_proj_kernel(
-    me_ref, bsame_ref, pre_ref, new_ref, back_ref, pick_ref, w_ref, own_ref, other_ref
-):
-    x, core = me_ref[0], me_ref[1]
-    length = pre_ref.shape[0]
-    chips = own_ref.shape[0]
-    pre = pre_ref[...]
-    first_head = lax.broadcasted_iota(jnp.int32, (new_ref.shape[0], 128), 1) < HD
-    got = jnp.dot(pick_ref[...], back_ref[...], preferred_element_type=F32)
-    total = jnp.where(
-        first_head, got[:, 128:129] + got[:, 130:131], got[:, 129:130] + got[:, 131:132]
-    )
-    qk = new_ref[:, 0:128].astype(F32) * new_ref[:, 128:256].astype(F32)
-    s0 = jnp.sum(jnp.where(first_head, qk, 0.0), axis=1, keepdims=True)
-    s1 = jnp.sum(jnp.where(first_head, 0.0, qk), axis=1, keepdims=True)
-    own = jnp.where(
-        first_head,
-        jnp.exp(s0 * (HD**-0.5) + bsame_ref[0]),
-        jnp.exp(s1 * (HD**-0.5) + bsame_ref[1]),
-    )
-    value = new_ref[:, 256:384].astype(F32)
-    dec = ((got[:, 0:128] * total + own * value) / (total + own)).astype(BF)
-    for away in range(chips):
-        chip = lax.rem(x + away, chips)
-        w = w_ref[pl.ds(pl.multiple_of(chip * 256, 256), 256), :]
-        for left, start, size in ((pre, 0, length), (dec, length, dec.shape[0])):
-            o = dot_nt(left, w).astype(BF)
-            own_ref[away, start : start + size, :] = jnp.where(core == 0, o[:, :128], o[:, 128:])
-            other_ref[away, start : start + size, :] = jnp.where(core == 0, o[:, 128:], o[:, :128])
-
-
-def out_proj_call(me, bsame, pre, qkv, back, pick, big, col_block):
-    length = pre.shape[0]
-    rows = length + pick.shape[0]
-    width = big.shape[0]
-    chips = width // 256
-    half = jax.ShapeDtypeStruct((chips, rows, 128), BF)
-    return pl.pallas_call(
-        out_proj_kernel,
-        grid=(1,),
-        in_specs=[
-            pl.BlockSpec(memory_space=pltpu.SMEM),
-            pl.BlockSpec(memory_space=pltpu.SMEM),
-            whole(pre.shape),
-            pl.BlockSpec((pick.shape[0], 384), lambda i: (length // pick.shape[0], 0)),
-            whole(back.shape),
-            whole(pick.shape),
-            pl.BlockSpec((width, 128), lambda i: (0, col_block)),
-        ],
-        out_specs=[whole(half.shape), whole(half.shape)],
-        out_shape=[half, half],
-        cost_estimate=pl.CostEstimate(
-            flops=2 * rows * 128 * width, bytes_accessed=2 * 1024 * 1024, transcendentals=0
-        ),
-        name="out_proj",
-    )(me, bsame, pre, qkv, back, pick, big)
 
 
 def ffn_kernel(me_ref, ra_ref, rb_ref, norm_ref, gate_ref, up_ref, down_ref, own_ref, other_ref):
@@ -391,23 +420,29 @@
     )(me, ra, rb, norm2, big, big, big)
 
 
-def tail_kernel(target_ref, row_ref, new_ref, pages_ref, out_ref, sem):
-    count = out_ref.shape[0]
-    copies = [
-        pltpu.make_async_copy(pages_ref.at[target_ref[r]], out_ref.at[r], sem.at[r])
+def tail_kernel(target_ref, row_ref, new_ref, pages_ref, out_ref, buf, in_sem, out_sem):
+    count = buf.shape[0]
+    reads = [
+        pltpu.make_async_copy(pages_ref.at[target_ref[r]], buf.at[r], in_sem.at[r])
         for r in range(count)
     ]
-    for c in copies:
+    writes = [
+        pltpu.make_async_copy(buf.at[r], out_ref.at[r], out_sem.at[r]) for r in range(count)
+    ]
+    for c in reads:
         c.start()
     for r in range(count):
-        copies[r].wait()
+        reads[r].wait()
         row = row_ref[r]
         start = pl.multiple_of((row // 16) * 16, 16)
         hit = lax.broadcasted_iota(jnp.int32, (16, 128), 0) == row - start
         for i in range(2):
-            new = new_ref[r : r + 1, (1 + i) * 128 : (2 + i) * 128].astype(F32)
-            old = out_ref[r, i, pl.ds(start, 16), :].astype(F32)
-            out_ref[r, i, pl.ds(start, 16), :] = jnp.where(hit, new, old).astype(BF)
+            new = new_ref[r : r + 1, i * 128 : (i + 1) * 128].astype(F32)
+            old = buf[r, i, pl.ds(start, 16), :].astype(F32)
+            buf[r, i, pl.ds(start, 16), :] = jnp.where(hit, new, old).astype(BF)
+        writes[r].start()
+    for c in writes:
+        c.wait()
 
 
 def tail_call(target, row, new, pages):
@@ -420,12 +455,16 @@
         in_specs=[
             smem,
             smem,
-            pl.BlockSpec((count, 384), lambda i: (new.shape[0] // count - 1, 0)),
+            whole(new.shape),
             pl.BlockSpec(memory_space=pl.ANY),
         ],
-        out_specs=whole(shape),
+        out_specs=pl.BlockSpec(memory_space=pl.ANY),
         out_shape=jax.ShapeDtypeStruct(shape, BF),
-        scratch_shapes=[pltpu.SemaphoreType.DMA((count,))],
+        scratch_shapes=[
+            pltpu.VMEM(shape, BF),
+            pltpu.SemaphoreType.DMA((count,)),
+            pltpu.SemaphoreType.DMA((count,)),
+        ],
         cost_estimate=pl.CostEstimate(
             flops=0, bytes_accessed=4 * 1024 * 1024, transcendentals=0
         ),
@@ -499,14 +538,18 @@
     row_at = lax.axis_index("row")
     me = jnp.stack([row_at // 2, row_at % 2]).astype(jnp.int32)
 
-    sent = pack_call(dec_table, dec_len, dec_variate, dec_holder, layer_input, w_q, peers)
+    sent, wide = pack_call(
+        dec_table.T,
+        dec_len,
+        dec_variate,
+        dec_holder.T,
+        layer_input,
+        w_q,
+        peers,
+        (w_gate, w_up, w_down.T, w_o.T, w_k, w_v),
+    )
     got = exchange(sent, "col")
-    big = lax.all_gather(
-        jnp.concatenate([w_gate, w_up, w_down.T, w_o.T, w_k, w_v], axis=1),
-        "col",
-        axis=0,
-        tiled=True,
-    )
+    big = lax.all_gather(wide, "col", axis=0, tiled=True)
     xa, xb = row_gather(layer_input, chips)
 
     slot_rows = got[:, -8 : 2 * slots - 8]
@@ -546,53 +589,46 @@
         kv_pool,
         page_variates,
     )
-    back = exchange(dec.reshape(peers, slots, 2 * width), "col").reshape(
-        peers * slots, 2 * width
-    )
-    old_tails, back = lax.optimization_barrier((old_tails, back))
-    tails = exchange(old_tails, "col")
+    back = exchange(dec, "col").reshape(peers * 8, width)
 
     holder = dec_holder[:, 0]
     earlier = jnp.arange(dec_count)[:, None] > jnp.arange(dec_count)[None, :]
     rank = jnp.sum(((holder[:, None] == holder[None, :]) & earlier).astype(jnp.int32), axis=1)
     target = holder * slots + rank
-    pick = (target[:, None] == jnp.arange(peers * slots)[None, :]).astype(BF)
+    places = jnp.arange(peers * 8)[None, :]
+    pick = (places == (holder * 8 + rank)[:, None]).astype(BF)
+    picksum = (places == (holder * 8 + rank + slots)[:, None]).astype(BF)
     variates = pre_variate[0]
     starts = jnp.sum((variates[None, :] < variates[:, None]).astype(jnp.int32), axis=1)
     cos, sin = turns(jnp.concatenate([jnp.arange(pre_len) - starts, dec_len]))
 
-    qkv = qkv_call(
+    old_tails, back, cos, sin = lax.optimization_barrier((old_tails, back, cos, sin))
+    tails = exchange(old_tails, "col")
+    normed, q = early_call(me, xa, xb, norm1[None], got, cos, sin, q_gain[None])
+    new, prefill_pages, own, other = attn_call(
         me,
-        xa,
-        xb,
-        norm1[None],
-        got,
+        bias_same,
+        bias_diff,
+        normed,
+        q,
         big,
-        3 * hidden // width + 1,
+        3 * hidden // width,
         cos,
         sin,
-        q_gain[None],
         k_gain[None],
-    )
-    pre_out, prefill_pages = prefill_call(
-        qkv,
         pre_variate.reshape(pre_len, 1),
         pre_variate,
         pre_keep,
-        bias_same,
-        bias_diff,
-        pre_len,
-        page,
-    )
-    own, other = out_proj_call(
-        me, bias_same, pre_out, qkv, back, pick, big, 3 * hidden // width
+        back,
+        pick,
+        picksum,
     )
     resid = layer_input.astype(F32) + row_scatter(own, other)
     ra, rb = row_gather(resid.astype(BF), chips)
     own, other = ffn_call(me, ra, rb, norm2[None], big, hidden)
     out = (resid + row_scatter(own, other)).astype(BF)
     tail_pages = tail_call(
-        target, dec_len % page, qkv, tails.reshape(peers * slots, 2, page, width)
+        target, dec_len % page, new, tails.reshape(peers * slots, 2, page, width)
     )
     return (out, prefill_pages, tail_pages)
 

time: 196 us -> 191 us (0.974)
  local copies, waits for them, and re-layouts: 14.6 us -> 6.28 us
  starting transfers between devices: 36.6 us -> 44.1 us
  waiting for transfers between devices: 95.3 us -> 91 us
    all_to_all x3, waiting for transfers between devices: 38.9 us -> 22.1 us  [exchange(): return lax.all_to_all(x, axis, split_axis=0, concat_axis=0, tiled=True)]
    all_gather x1, waiting for transfers between devices: 26.1 us -> 40.3 us  [on_device(): big = lax.all_gather(wide, 'col', axis=0, tiled=True)]
    ppermute x20, starting transfers between devices: 14.6 us -> 22.5 us  [shifted(): return lax.ppermute(x, axis, pairs)]
    unnamed x37 -> x30, local copies, waits for them, and re-layouts: 7.7 us -> 2.08 us
    reshape x2 -> x0, local copies, waits for them, and re-layouts: 2.02 us -> none  [the longest x1 1.39 us: on_device(): dec.reshape(peers, slots, 2 * width)]
    pallas_call x4 -> x3, Pallas kernels: 14.9 us -> 14 us  [the longest x1 7 us: attn_call(): pl.pallas_call(attn_kernel, grid=(1,), in_specs=[smem, smem, smem, whole(...]
  transfers between devices with their start and end apart: 24 -> 24, of which waited for: 18 -> 20; matrix products, arithmetic and copies ran while one was open for 8% -> 6% of each run, Pallas kernels for 13% -> 12%
where the time goes in v2:
time: 191 us; the launch traced here: 189 us
  waiting for transfers between devices  91 us (48%)
  starting transfers between devices  44.1 us (23%)
  Pallas kernels  25.2 us (13%)
  between operations  14.4 us (8%)
  other arithmetic  7.88 us (4%)
  local copies, waits for them, and re-layouts  6.28 us (3%)
    all_gather x1, waiting for transfers between devices, on_device(): big = lax.all_gather(wide, 'col', axis=0, tiled=True)  40.3 us
    ppermute x20, waiting for transfers between devices, shifted(): return lax.ppermute(x, axis, pairs)  28.6 us
    ppermute x20, starting transfers between devices, shifted(): return lax.ppermute(x, axis, pairs)  22.5 us
    all_to_all x3, waiting for transfers between devices, exchange(): return lax.all_to_all(x, axis, split_axis=0, concat_axis=0, tiled=True)  22.1 us
    all_to_all x3, starting transfers between devices, exchange(): return lax.all_to_all(x, axis, split_axis=0, concat_axis=0, tiled=True)  21.6 us
    pallas_call x1, Pallas kernels, attn_call(): pl.pallas_call(attn_kernel, grid=(1,), in_specs=[smem, smem, smem, whole(...  7 us
    pallas_call x1, Pallas kernels, decode_call(): pl.pallas_call(decode_kernel, grid=(1,), in_specs=[smem if i in (0, 9, 10...  5.24 us
    pallas_call x1, Pallas kernels, early_call(): pl.pallas_call(early_kernel, grid=(3,), in_specs=[pl.BlockSpec(memory_spa...  4.14 us
  transfers between devices with their start and end apart: 24, of which 20 were waited for; matrix products, arithmetic and copies ran while one was open for 6% of the time, Pallas kernels for 12%

profile of v2, /device:TPU:38, one launch (start us, length us, event | category | flops | bytes accessed | tf_op | source)
XLA Modules:
  0.0 188.8 jit_solution(17469974432775704961)
XLA Ops:
  7.2 2.0 %pack.1 = (bf16[32,40,128]{2,1,0:T(8,128)(2,1)}, bf16[32,1920]{1,0:T(8,128)(2,1)}) custom-call(s32[8,16]{1,0:T(8,128)} %bitcast.111, s32[16]{0:T(128)} %len_ref.1, s32[16]{0:T(128)} %var_ref.1, s32[1,16]{1,0:T(1,128)} %bitcast.109, bf16[528,128]{1,0:T(8,128)(2,1)} %x_ref.1, bf16[32,128]{1,0:T(8,128)(2,1)} %w_ref.1, bf16[32,512]{1,0:T(8,128)(2,1)} %refs_0_.1, ...), custom_call_target="tpu_custom_call" | custom-call | bytes 1048576 | tf_op jit(solution)/shard_map/pack/pallas_call | solution.py:94
  9.2 11.4 %all-to-all-start = ((bf16[32,40,128]{2,1,0:T(8,128)(2,1)}), bf16[32,40,128]{2,1,0:T(8,128)(2,1)S(1)}, u32[]{:S(2)}, u32[]{:S(2)}) async-start(bf16[32,40,128]{2,1,0:T(8,128)(2,1)} %get-tuple-element.17), calls=%async_computation | async-start | bytes 655360 | tf_op jit(solution)/shard_map/all_to_all | solution.py:501
  21.5 1.9 fusion
  23.3 10.7 %all-to-all-done.w_ref.wq_ref = bf16[32,40,128]{2,1,0:T(8,128)(2,1)S(1)} async-done(((bf16[32,40,128]{2,1,0:T(8,128)(2,1)}), bf16[32,40,128]{2,1,0:T(8,128)(2,1)S(1)}, u32[]{:S(2)}, u32[]{:S(2)}) %all-to-all-start) | async-done | bytes 327712 | tf_op jit(solution)/shard_map/all_to_all | solution.py:501
  34.6 2.4 %collective-permute-start.5 = (bf16[64,128]{1,0:T(8,128)(2,1)S(1)}, bf16[64,128]{1,0:T(8,128)(2,1)S(1)}, u32[]{:S(2)}, u32[]{:S(2)}) collective-permute-start(bf16[64,128]{1,0:T(8,128)(2,1)S(1)} %bitcast.97), channel_id=1, source_target_pairs={{0,128},{32,160},{64,192},{96,224},{128,0},{160,32},{192,64},{224,... | collective-permute-start | bytes 49160 | tf_op jit(solution)/shard_map/ppermute | solution.py:482
  38.3 1.5 collective-permute-done.5
  39.9 2.2 %collective-permute-done.6 = bf16[64,128]{1,0:T(8,128)(2,1)S(1)} collective-permute-done((bf16[64,128]{1,0:T(8,128)(2,1)S(1)}, bf16[64,128]{1,0:T(8,128)(2,1)S(1)}, u32[]{:S(2)}, u32[]{:S(2)}) %collective-permute-start.6) | collective-permute-done | bytes 16416 | tf_op jit(solution)/shard_map/ppermute | solution.py:482
  44.0 5.2 %decode.1 = bf16[32,8,128]{2,1,0:T(8,128)(2,1)} custom-call(s32[2]{0:T(128)} %pad_add_fusion.me_ref, bf16[4,64,128]{2,1,0:T(8,128)(2,1)} %copy-done.10, bf16[4,64,128]{2,1,0:T(8,128)(2,1)} %copy-done.11, f32[1,1024]{1,0:T(1,128)} %bitcast.103, bf16[32,40,128]{2,1,0:T(8,128)(2,1)} %copy-done.4, f32[64,128]{1,0:T(8,128)} %get-tuple-element.46.cos_ref, ...), custom_call_target="tpu_custom_call" | custom-call | flops 268435456 | bytes 3145728 | tf_op jit(solution)/shard_map/decode/pallas_call | solution.py:364
  49.3 4.6 %all-to-all-start.1 = ((bf16[32,8,128]{2,1,0:T(8,128)(2,1)}), bf16[32,8,128]{2,1,0:T(8,128)(2,1)S(1)}, u32[]{:S(2)}, u32[]{:S(2)}) async-start(bf16[32,8,128]{2,1,0:T(8,128)(2,1)} %decode.1), calls=%async_computation.1 | async-start | bytes 131072 | tf_op jit(solution)/shard_map/all_to_all | solution.py:501
  54.0 3.1 %gather_fusion = bf16[64,2,128,128]{3,2,1,0:T(8,128)(2,1)} fusion(bf16[32,2,128,128]{3,2,1,0:T(8,128)(2,1)S(1)} %copy-done.3, s32[1024]{0:T(1024)S(1)} %pad_clamp_fusion), kind=kCustom, calls=%fused_computation | custom fusion | bytes 8388864 | tf_op jit(solution)/shard_map/gather | solution.py:565
  57.0 6.0 %all-to-all-done.1 = bf16[32,8,128]{2,1,0:T(8,128)(2,1)S(1)} async-done(((bf16[32,8,128]{2,1,0:T(8,128)(2,1)}), bf16[32,8,128]{2,1,0:T(8,128)(2,1)S(1)}, u32[]{:S(2)}, u32[]{:S(2)}) %all-to-all-start.1) | async-done | bytes 65568 | tf_op jit(solution)/shard_map/all_to_all | solution.py:501
  63.6 5.6 %all-to-all-start.2 = ((bf16[32,2,2,128,128]{4,3,2,1,0:T(8,128)(2,1)}), bf16[32,2,2,128,128]{4,3,2,1,0:T(8,128)(2,1)}, u32[]{:S(2)}, u32[]{:S(2)}) async-start(bf16[32,2,2,128,128]{4,3,2,1,0:T(8,128)(2,1)} %bitcast.85), calls=%async_computation.2 | async-start | bytes 8388608 | tf_op jit(solution)/shard_map/all_to_all | solution.py:501
  72.2 2.5 %collective-permute-done = bf16[528,128]{1,0:T(8,128)(2,1)S(1)} collective-permute-done((bf16[528,128]{1,0:T(8,128)(2,1)S(1)}, bf16[528,128]{1,0:T(8,128)(2,1)S(1)}, u32[]{:S(2)}, u32[]{:S(2)}) %collective-permute-start) | collective-permute-done | bytes 135200 | tf_op jit(solution)/shard_map/ppermute | solution.py:482
  74.7 2.2 %collective-permute-done.1 = bf16[528,128]{1,0:T(8,128)(2,1)S(1)} collective-permute-done((bf16[528,128]{1,0:T(8,128)(2,1)S(1)}, bf16[528,128]{1,0:T(8,128)(2,1)S(1)}, u32[]{:S(2)}, u32[]{:S(2)}) %collective-permute-start.1) | collective-permute-done | bytes 135200 | tf_op jit(solution)/shard_map/ppermute | solution.py:482
  81.3 4.1 %early.1 = (bf16[528,1024]{1,0:T(8,128)(2,1)}, bf16[528,128]{1,0:T(8,128)(2,1)}) custom-call(s32[2]{0:T(128)} %pad_add_fusion.me_ref, bf16[4,528,128]{2,1,0:T(8,128)(2,1)} %copy-done.5, bf16[4,528,128]{2,1,0:T(8,128)(2,1)} %copy-done.8, f32[1,1024]{1,0:T(1,128)} %bitcast.104, bf16[32,40,128]{2,1,0:T(8,128)(2,1)} %copy-done.4, ...), custom_call_target="tpu_custom_call" | custom-call | flops 138412032 | bytes 4194304 | tf_op jit(solution)/shard_map/early/pallas_call | solution.py:129
  85.4 40.3 %all-gather.2.cloned.1.call-done.wk_ref.wv_ref.wo_ref.gate_ref.up_ref.down_ref = bf16[1024,1920]{1,0:T(8,128)(2,1)} async-done(((bf16[32,1920]{1,0:T(8,128)(2,1)}), bf16[1024,1920]{1,0:T(8,128)(2,1)}) %all-gather.2.cloned.1.call-update) | async-done | bytes 3932176 | tf_op jit(solution)/shard_map/all_gather | solution.py:552
  125.7 7.0 %attn.1 = (bf16[16,256]{1,0:T(8,128)(2,1)}, bf16[4,2,128,128]{3,2,1,0:T(8,128)(2,1)}, bf16[4,528,128]{2,1,0:T(8,128)(2,1)}, bf16[4,528,128]{2,1,0:T(8,128)(2,1)}) custom-call(s32[2]{0:T(128)} %pad_add_fusion.me_ref, f32[2]{0:T(128)} %bsame_ref.3, f32[2]{0:T(128)} %bdiff_ref.3, bf16[528,1024]{1,0:T(8,128)(2,1)} %get-tuple-element.20.normed_ref, ...), custom_call_target="tpu_custom_call" | custom-call | flops 683671552 | bytes 6291456 | tf_op jit(solution)/shard_map/attn/pallas_call | solution.py:260
  132.7 2.1 %collective-permute-done.8 = bf16[4,528,128]{2,1,0:T(8,128)(2,1)S(1)} collective-permute-done((bf16[4,528,128]{2,1,0:T(8,128)(2,1)}, bf16[4,528,128]{2,1,0:T(8,128)(2,1)S(1)}, u32[]{:S(2)}, u32[]{:S(2)}) %collective-permute-start.8) | collective-permute-done | bytes 540704 | tf_op jit(solution)/shard_map/ppermute | solution.py:482
  136.2 5.1 %collective-permute-start.10 = (bf16[528,128]{1,0:T(8,128)(2,1)S(1)}, bf16[528,128]{1,0:T(8,128)(2,1)S(1)}, u32[]{:S(2)}, u32[]{:S(2)}) collective-permute-start(bf16[528,128]{1,0:T(8,128)(2,1)S(1)} %get-tuple-element.40), channel_id=1, source_target_pairs={{0,128},{32,160},{64,192},{96,224},{128,0},{160,32},{192,64},{224,... | collective-permute-start | bytes 405512 | tf_op jit(solution)/shard_map/ppermute | solution.py:482
  141.4 3.1 %collective-permute-start.9 = (bf16[528,128]{1,0:T(8,128)(2,1)S(1)}, bf16[528,128]{1,0:T(8,128)(2,1)S(1)}, u32[]{:S(2)}, u32[]{:S(2)}) collective-permute-start(bf16[528,128]{1,0:T(8,128)(2,1)S(1)} %get-tuple-element.38), channel_id=1, source_target_pairs={{0,64},{32,96},{64,128},{96,160},{128,192},{160,224},{192,0},{224,... | collective-permute-start | bytes 405512 | tf_op jit(solution)/shard_map/ppermute | solution.py:482
  145.3 2.8 %collective-permute-done.11 = bf16[528,128]{1,0:T(8,128)(2,1)S(1)} collective-permute-done((bf16[528,128]{1,0:T(8,128)(2,1)S(1)}, bf16[528,128]{1,0:T(8,128)(2,1)S(1)}, u32[]{:S(2)}, u32[]{:S(2)}) %collective-permute-start.11) | collective-permute-done | bytes 135200 | tf_op jit(solution)/shard_map/ppermute | solution.py:482
  148.2 3.0 %collective-permute-start.12 = (bf16[528,128]{1,0:T(8,128)(2,1)S(1)}, bf16[528,128]{1,0:T(8,128)(2,1)S(1)}, u32[]{:S(2)}, u32[]{:S(2)}) collective-permute-start(bf16[528,128]{1,0:T(8,128)(2,1)S(1)} %fusion.26), channel_id=1, source_target_pairs={{0,64},{32,96},{64,128},{96,160},{128,192},{160,224},{192,0},{224,... | collective-permute-start | bytes 405512 | tf_op jit(solution)/shard_map/ppermute | solution.py:482
  151.2 2.4 %collective-permute-start.13 = (bf16[528,128]{1,0:T(8,128)(2,1)S(1)}, bf16[528,128]{1,0:T(8,128)(2,1)S(1)}, u32[]{:S(2)}, u32[]{:S(2)}) collective-permute-start(bf16[528,128]{1,0:T(8,128)(2,1)S(1)} %fusion.26), channel_id=1, source_target_pairs={{0,128},{32,160},{64,192},{96,224},{128,0},{160,32},{192,64},{224,... | collective-permute-start | bytes 405512 | tf_op jit(solution)/shard_map/ppermute | solution.py:482
  153.6 2.3 %collective-permute-done.12 = bf16[528,128]{1,0:T(8,128)(2,1)S(1)} collective-permute-done((bf16[528,128]{1,0:T(8,128)(2,1)S(1)}, bf16[528,128]{1,0:T(8,128)(2,1)S(1)}, u32[]{:S(2)}, u32[]{:S(2)}) %collective-permute-start.12) | collective-permute-done | bytes 135200 | tf_op jit(solution)/shard_map/ppermute | solution.py:482
  155.9 3.3 %collective-permute-done.13 = bf16[528,128]{1,0:T(8,128)(2,1)S(1)} collective-permute-done((bf16[528,128]{1,0:T(8,128)(2,1)S(1)}, bf16[528,128]{1,0:T(8,128)(2,1)S(1)}, u32[]{:S(2)}, u32[]{:S(2)}) %collective-permute-start.13) | collective-permute-done | bytes 135200 | tf_op jit(solution)/shard_map/ppermute | solution.py:482
  159.2 1.8 collective-permute-done.14
  161.2 1.9 %collective-permute-done.15.rb_ref = bf16[4,528,128]{2,1,0:T(8,128)(2,1)S(1)} collective-permute-done((bf16[4,528,128]{2,1,0:T(8,128)(2,1)S(1)}, bf16[4,528,128]{2,1,0:T(8,128)(2,1)S(1)}, u32[]{:S(2)}, u32[]{:S(2)}) %collective-permute-start.15) | collective-permute-done | bytes 540704 | tf_op jit(solution)/shard_map/ppermute | solution.py:482
  163.1 4.0 %ffn.1 = (bf16[4,528,128]{2,1,0:T(8,128)(2,1)S(1)}, bf16[4,528,128]{2,1,0:T(8,128)(2,1)S(1)}) custom-call(s32[2]{0:T(128)S(1)} %copy-done.1, bf16[4,528,128]{2,1,0:T(8,128)(2,1)S(1)} %pad_maximum_fusion.1.ra_ref, bf16[4,528,128]{2,1,0:T(8,128)(2,1)S(1)} %collective-permute-done.15.rb_ref, f32[1,1024]{1,0:T(1,128)S(1)} %bitcast.84, ...), custom_call_target="tpu_custom_call" | custom-call | flops 1660944384 | bytes 6291456 | tf_op jit(solution)/shard_map/ffn/pallas_call | solution.py:401
  167.3 1.8 collective-permute-done.16
  169.5 2.8 %collective-permute-start.18 = (bf16[528,128]{1,0:T(8,128)(2,1)S(1)}, bf16[528,128]{1,0:T(8,128)(2,1)S(1)}, u32[]{:S(2)}, u32[]{:S(2)}) collective-permute-start(bf16[528,128]{1,0:T(8,128)(2,1)S(1)} %get-tuple-element.37), channel_id=1, source_target_pairs={{0,128},{32,160},{64,192},{96,224},{128,0},{160,32},{192,64},{224,... | collective-permute-start | bytes 405512 | tf_op jit(solution)/shard_map/ppermute | solution.py:482
  172.9 5.4 %all-to-all-done.2 = bf16[32,2,2,128,128]{4,3,2,1,0:T(8,128)(2,1)} async-done(((bf16[32,2,2,128,128]{4,3,2,1,0:T(8,128)(2,1)}), bf16[32,2,2,128,128]{4,3,2,1,0:T(8,128)(2,1)}, u32[]{:S(2)}, u32[]{:S(2)}) %all-to-all-start.2) | async-done | bytes 4194336 | tf_op jit(solution)/shard_map/all_to_all | solution.py:501
  178.3 2.9 %tail.1 = bf16[16,2,128,128]{3,2,1,0:T(8,128)(2,1)} custom-call(s32[16]{0:T(128)} %get-tuple-element.52.target_ref, s32[16]{0:T(128)} %get-tuple-element.51.row_ref, bf16[16,256]{1,0:T(8,128)(2,1)} %get-tuple-element.29.new_ref, bf16[64,2,128,128]{3,2,1,0:T(8,128)(2,1)} %bitcast.43.pages_ref), custom_call_target="tpu_custom_call" | custom-call | bytes 4194304 | tf_op jit(solution)/shard_map/tail/pallas_call | solution.py:452
  (83 shorter events, 17.2 us)
Async XLA Ops:
  7.2 14.3 %copy-start.14 = (s32[16]{0:T(128)S(1)}, s32[16]{0:T(128)}, u32[]{:S(2)}) copy-start(s32[16]{0:T(128)} %len_ref.1) | copy-start | bytes 196
  7.2 13.5 %copy-start.12 = (s32[1,512]{1,0:T(1,128)S(1)}, s32[1,512]{1,0:T(1,128)}, u32[]{:S(2)}) copy-start(s32[1,512]{1,0:T(1,128)} %vrow_ref.1) | copy-start | bytes 6148
  7.2 118.5 %all-gather.2.cloned.1.call-start = ((), (), s32[]{:S(2)}) async-start(), calls=%async_computation.3 | async-start | bytes 4055040 | tf_op jit(solution)/shard_map/all_gather | solution.py:552
  9.2 24.8 %all-to-all-start = ((bf16[32,40,128]{2,1,0:T(8,128)(2,1)}), bf16[32,40,128]{2,1,0:T(8,128)(2,1)S(1)}, u32[]{:S(2)}, u32[]{:S(2)}) async-start(bf16[32,40,128]{2,1,0:T(8,128)(2,1)} %get-tuple-element.17), calls=%async_computation | async-start | bytes 655360 | tf_op jit(solution)/shard_map/all_to_all | solution.py:501
  34.0 9.4 %copy-start.4 = (bf16[32,40,128]{2,1,0:T(8,128)(2,1)}, bf16[32,40,128]{2,1,0:T(8,128)(2,1)S(1)}, u32[]{:S(2)}) copy-start(bf16[32,40,128]{2,1,0:T(8,128)(2,1)S(1)} %all-to-all-done.w_ref.wq_ref) | copy-start | bytes 983044
  34.1 4.3 %collective-permute-start.4 = (bf16[64,128]{1,0:T(8,128)(2,1)S(1)}, bf16[64,128]{1,0:T(8,128)(2,1)S(1)}, u32[]{:S(2)}, u32[]{:S(2)}) collective-permute-start(bf16[64,128]{1,0:T(8,128)(2,1)S(1)} %bitcast.96), channel_id=1, source_target_pairs={{0,64},{32,96},{64,128},{96,160},{128,192},{160,224},{192,0},{224,... | collective-permute-start | bytes 49160 | tf_op jit(solution)/shard_map/ppermute | solution.py:482
  34.6 5.2 %collective-permute-start.5 = (bf16[64,128]{1,0:T(8,128)(2,1)S(1)}, bf16[64,128]{1,0:T(8,128)(2,1)S(1)}, u32[]{:S(2)}, u32[]{:S(2)}) collective-permute-start(bf16[64,128]{1,0:T(8,128)(2,1)S(1)} %bitcast.97), channel_id=1, source_target_pairs={{0,128},{32,160},{64,192},{96,224},{128,0},{160,32},{192,64},{224,... | collective-permute-start | bytes 49160 | tf_op jit(solution)/shard_map/ppermute | solution.py:482
  37.1 4.9 %collective-permute-start.6 = (bf16[64,128]{1,0:T(8,128)(2,1)S(1)}, bf16[64,128]{1,0:T(8,128)(2,1)S(1)}, u32[]{:S(2)}, u32[]{:S(2)}) collective-permute-start(bf16[64,128]{1,0:T(8,128)(2,1)S(1)} %bitcast.98), channel_id=1, source_target_pairs={{0,192},{32,224},{64,0},{96,32},{128,64},{160,96},{192,128},{224,1... | collective-permute-start | bytes 49160 | tf_op jit(solution)/shard_map/ppermute | solution.py:482
  42.1 1.3 collective-permute-start.7
  44.0 9.9 %copy-start.3 = (bf16[32,2,128,128]{3,2,1,0:T(8,128)(2,1)S(1)}, bf16[32,2,128,128]{3,2,1,0:T(8,128)(2,1)}, u32[]{:S(2)}) copy-start(bf16[32,2,128,128]{3,2,1,0:T(8,128)(2,1)} %pool_ref.1) | copy-start | bytes 6291460
  49.3 13.7 %all-to-all-start.1 = ((bf16[32,8,128]{2,1,0:T(8,128)(2,1)}), bf16[32,8,128]{2,1,0:T(8,128)(2,1)S(1)}, u32[]{:S(2)}, u32[]{:S(2)}) async-start(bf16[32,8,128]{2,1,0:T(8,128)(2,1)} %decode.1), calls=%async_computation.1 | async-start | bytes 131072 | tf_op jit(solution)/shard_map/all_to_all | solution.py:501
  63.6 114.7 %all-to-all-start.2 = ((bf16[32,2,2,128,128]{4,3,2,1,0:T(8,128)(2,1)}), bf16[32,2,2,128,128]{4,3,2,1,0:T(8,128)(2,1)}, u32[]{:S(2)}, u32[]{:S(2)}) async-start(bf16[32,2,2,128,128]{4,3,2,1,0:T(8,128)(2,1)} %bitcast.85), calls=%async_computation.2 | async-start | bytes 8388608 | tf_op jit(solution)/shard_map/all_to_all | solution.py:501
  69.2 9.3 %copy-start.13 = (s32[16,1]{0,1:T(1,128)S(1)}, s32[16,1]{0,1:T(1,128)}, u32[]{:S(2)}) copy-start(s32[16,1]{0,1:T(1,128)} %param.41) | copy-start | bytes 196
  69.2 5.5 %collective-permute-start = (bf16[528,128]{1,0:T(8,128)(2,1)S(1)}, bf16[528,128]{1,0:T(8,128)(2,1)S(1)}, u32[]{:S(2)}, u32[]{:S(2)}) collective-permute-start(bf16[528,128]{1,0:T(8,128)(2,1)S(1)} %copy-done.6), channel_id=1, source_target_pairs={{0,64},{32,96},{64,128},{96,160},{128,192},{160,224},{192,0},{224,... | collective-permute-start | bytes 405512 | tf_op jit(solution)/shard_map/ppermute | solution.py:482
  69.9 7.0 %collective-permute-start.1 = (bf16[528,128]{1,0:T(8,128)(2,1)S(1)}, bf16[528,128]{1,0:T(8,128)(2,1)S(1)}, u32[]{:S(2)}, u32[]{:S(2)}) collective-permute-start(bf16[528,128]{1,0:T(8,128)(2,1)S(1)} %copy-done.6), channel_id=1, source_target_pairs={{0,128},{32,160},{64,192},{96,224},{128,0},{160,32},{192,64},{224,... | collective-permute-start | bytes 405512 | tf_op jit(solution)/shard_map/ppermute | solution.py:482
  70.8 7.4 %collective-permute-start.2 = (bf16[528,128]{1,0:T(8,128)(2,1)S(1)}, bf16[528,128]{1,0:T(8,128)(2,1)S(1)}, u32[]{:S(2)}, u32[]{:S(2)}) collective-permute-start(bf16[528,128]{1,0:T(8,128)(2,1)S(1)} %copy-done.6), channel_id=1, source_target_pairs={{0,192},{32,224},{64,0},{96,32},{128,64},{160,96},{192,128},{224,1... | collective-permute-start | bytes 405512 | tf_op jit(solution)/shard_map/ppermute | solution.py:482
  78.3 2.2 %collective-permute-start.3 = (bf16[4,528,128]{2,1,0:T(8,128)(2,1)S(1)}, bf16[4,528,128]{2,1,0:T(8,128)(2,1)S(1)}, u32[]{:S(2)}, u32[]{:S(2)}) collective-permute-start(bf16[4,528,128]{2,1,0:T(8,128)(2,1)S(1)} %pad_maximum_fusion.xa_ref), channel_id=1, source_target_pairs={{0,32},{32,0},{64,96},{96,64},{128,160},{160,128},{192,224},{224,1... | collective-permute-start | bytes 1622024 | tf_op jit(solution)/shard_map/ppermute | solution.py:482
  132.7 2.1 %collective-permute-start.8 = (bf16[4,528,128]{2,1,0:T(8,128)(2,1)}, bf16[4,528,128]{2,1,0:T(8,128)(2,1)S(1)}, u32[]{:S(2)}, u32[]{:S(2)}) collective-permute-start(bf16[4,528,128]{2,1,0:T(8,128)(2,1)} %get-tuple-element.25), channel_id=1, source_target_pairs={{0,32},{32,0},{64,96},{96,64},{128,160},{160,128},{192,224},{224,1... | collective-permute-start | bytes 1622024 | tf_op jit(solution)/shard_map/ppermute | solution.py:482
  134.8 28.3 %copy-start = (bf16[1024,1920]{1,0:T(8,128)(2,1)S(1)}, bf16[1024,1920]{1,0:T(8,128)(2,1)}, u32[]{:S(2)}) copy-start(bf16[1024,1920]{1,0:T(8,128)(2,1)} %all-gather.2.cloned.1.call-done.wk_ref.wv_ref.wo_ref.gate_ref.up_ref.down_ref) | copy-start | bytes 11796484
  136.2 26.9 %copy-start.1 = (s32[2]{0:T(128)S(1)}, s32[2]{0:T(128)}, u32[]{:S(2)}) copy-start(s32[2]{0:T(128)} %pad_add_fusion.me_ref) | copy-start | bytes 28
  136.2 26.9 %copy-start.2 = (f32[1024]{0:T(1024)S(1)}, f32[1024]{0:T(1024)}, u32[]{:S(2)}) copy-start(f32[1024]{0:T(1024)} %param.31) | copy-start | bytes 12292
  136.2 9.1 %collective-permute-start.10 = (bf16[528,128]{1,0:T(8,128)(2,1)S(1)}, bf16[528,128]{1,0:T(8,128)(2,1)S(1)}, u32[]{:S(2)}, u32[]{:S(2)}) collective-permute-start(bf16[528,128]{1,0:T(8,128)(2,1)S(1)} %get-tuple-element.40), channel_id=1, source_target_pairs={{0,128},{32,160},{64,192},{96,224},{128,0},{160,32},{192,64},{224,... | collective-permute-start | bytes 405512 | tf_op jit(solution)/shard_map/ppermute | solution.py:482
  141.3 6.8 %collective-permute-start.11 = (bf16[528,128]{1,0:T(8,128)(2,1)S(1)}, bf16[528,128]{1,0:T(8,128)(2,1)S(1)}, u32[]{:S(2)}, u32[]{:S(2)}) collective-permute-start(bf16[528,128]{1,0:T(8,128)(2,1)S(1)} %get-tuple-element.39), channel_id=1, source_target_pairs={{0,192},{32,224},{64,0},{96,32},{128,64},{160,96},{192,128},{224,1... | collective-permute-start | bytes 405512 | tf_op jit(solution)/shard_map/ppermute | solution.py:482
  141.4 6.7 %collective-permute-start.9 = (bf16[528,128]{1,0:T(8,128)(2,1)S(1)}, bf16[528,128]{1,0:T(8,128)(2,1)S(1)}, u32[]{:S(2)}, u32[]{:S(2)}) collective-permute-start(bf16[528,128]{1,0:T(8,128)(2,1)S(1)} %get-tuple-element.38), channel_id=1, source_target_pairs={{0,64},{32,96},{64,128},{96,160},{128,192},{160,224},{192,0},{224,... | collective-permute-start | bytes 405512 | tf_op jit(solution)/shard_map/ppermute | solution.py:482
  148.2 7.7 %collective-permute-start.12 = (bf16[528,128]{1,0:T(8,128)(2,1)S(1)}, bf16[528,128]{1,0:T(8,128)(2,1)S(1)}, u32[]{:S(2)}, u32[]{:S(2)}) collective-permute-start(bf16[528,128]{1,0:T(8,128)(2,1)S(1)} %fusion.26), channel_id=1, source_target_pairs={{0,64},{32,96},{64,128},{96,160},{128,192},{160,224},{192,0},{224,... | collective-permute-start | bytes 405512 | tf_op jit(solution)/shard_map/ppermute | solution.py:482
  151.2 8.0 %collective-permute-start.13 = (bf16[528,128]{1,0:T(8,128)(2,1)S(1)}, bf16[528,128]{1,0:T(8,128)(2,1)S(1)}, u32[]{:S(2)}, u32[]{:S(2)}) collective-permute-start(bf16[528,128]{1,0:T(8,128)(2,1)S(1)} %fusion.26), channel_id=1, source_target_pairs={{0,128},{32,160},{64,192},{96,224},{128,0},{160,32},{192,64},{224,... | collective-permute-start | bytes 405512 | tf_op jit(solution)/shard_map/ppermute | solution.py:482
  153.6 7.4 %collective-permute-start.14 = (bf16[528,128]{1,0:T(8,128)(2,1)S(1)}, bf16[528,128]{1,0:T(8,128)(2,1)S(1)}, u32[]{:S(2)}, u32[]{:S(2)}) collective-permute-start(bf16[528,128]{1,0:T(8,128)(2,1)S(1)} %fusion.26), channel_id=1, source_target_pairs={{0,192},{32,224},{64,0},{96,32},{128,64},{160,96},{192,128},{224,1... | collective-permute-start | bytes 405512 | tf_op jit(solution)/shard_map/ppermute | solution.py:482
  161.1 2.0 %collective-permute-start.15 = (bf16[4,528,128]{2,1,0:T(8,128)(2,1)S(1)}, bf16[4,528,128]{2,1,0:T(8,128)(2,1)S(1)}, u32[]{:S(2)}, u32[]{:S(2)}) collective-permute-start(bf16[4,528,128]{2,1,0:T(8,128)(2,1)S(1)} %pad_maximum_fusion.1.ra_ref), channel_id=1, source_target_pairs={{0,32},{32,0},{64,96},{96,64},{128,160},{160,128},{192,224},{224,1... | collective-permute-start | bytes 1622024 | tf_op jit(solution)/shard_map/ppermute | solution.py:482
  167.1 2.0 %collective-permute-start.16 = (bf16[4,528,128]{2,1,0:T(8,128)(2,1)S(1)}, bf16[4,528,128]{2,1,0:T(8,128)(2,1)S(1)}, u32[]{:S(2)}, u32[]{:S(2)}) collective-permute-start(bf16[4,528,128]{2,1,0:T(8,128)(2,1)S(1)} %get-tuple-element.27), channel_id=1, source_target_pairs={{0,32},{32,0},{64,96},{96,64},{128,160},{160,128},{192,224},{224,1... | collective-permute-start | bytes 1622024 | tf_op jit(solution)/shard_map/ppermute | solution.py:482
  169.3 11.9 %collective-permute-start.17 = (bf16[528,128]{1,0:T(8,128)(2,1)S(1)}, bf16[528,128]{1,0:T(8,128)(2,1)S(1)}, u32[]{:S(2)}, u32[]{:S(2)}) collective-permute-start(bf16[528,128]{1,0:T(8,128)(2,1)S(1)} %get-tuple-element.35), channel_id=1, source_target_pairs={{0,64},{32,96},{64,128},{96,160},{128,192},{160,224},{192,0},{224,... | collective-permute-start | bytes 405512 | tf_op jit(solution)/shard_map/ppermute | solution.py:482
  169.5 11.7 %collective-permute-start.18 = (bf16[528,128]{1,0:T(8,128)(2,1)S(1)}, bf16[528,128]{1,0:T(8,128)(2,1)S(1)}, u32[]{:S(2)}, u32[]{:S(2)}) collective-permute-start(bf16[528,128]{1,0:T(8,128)(2,1)S(1)} %get-tuple-element.37), channel_id=1, source_target_pairs={{0,128},{32,160},{64,192},{96,224},{128,0},{160,32},{192,64},{224,... | collective-permute-start | bytes 405512 | tf_op jit(solution)/shard_map/ppermute | solution.py:482
  172.3 8.9 %collective-permute-start.19 = (bf16[528,128]{1,0:T(8,128)(2,1)S(1)}, bf16[528,128]{1,0:T(8,128)(2,1)S(1)}, u32[]{:S(2)}, u32[]{:S(2)}) collective-permute-start(bf16[528,128]{1,0:T(8,128)(2,1)S(1)} %get-tuple-element.36), channel_id=1, source_target_pairs={{0,192},{32,224},{64,0},{96,32},{128,64},{160,96},{192,128},{224,1... | collective-permute-start | bytes 405512 | tf_op jit(solution)/shard_map/ppermute | solution.py:482
  (7 other events, 18.1 us)
Sparse Core Ops, SparseCore 0:
  11.2 114.4 all-gather.1

commit v3 on v2

--- a/solution.py
+++ b/solution.py
@@ -627,8 +627,11 @@
     ra, rb = row_gather(resid.astype(BF), chips)
     own, other = ffn_call(me, ra, rb, norm2[None], big, hidden)
     out = (resid + row_scatter(own, other)).astype(BF)
+    out, tails, target, tail_row = lax.optimization_barrier(
+        (out, tails, target, dec_len % page)
+    )
     tail_pages = tail_call(
-        target, dec_len % page, new, tails.reshape(peers * slots, 2, page, width)
+        target, tail_row, new, tails.reshape(peers * slots, 2, page, width)
     )
     return (out, prefill_pages, tail_pages)
 

time: 191 us -> 193 us (1.010)
    ppermute x20, waiting for transfers between devices: 28.6 us -> 35.2 us  [shifted(): return lax.ppermute(x, axis, pairs)]
    all_to_all x3, waiting for transfers between devices: 22.1 us -> 16.7 us  [exchange(): return lax.all_to_all(x, axis, split_axis=0, concat_axis=0, tiled=True)]
  transfers between devices with their start and end apart: 24 -> 24, of which waited for: 20 -> 22; matrix products, arithmetic and copies ran while one was open for 6% -> 6% of each run, Pallas kernels for 12% -> 11%
where the time goes in v3:
time: 193 us; the launch traced here: 190 us
  waiting for transfers between devices  92.2 us (48%)
  starting transfers between devices  44.1 us (23%)
  Pallas kernels  25.2 us (13%)
  between operations  14.3 us (7%)
  other arithmetic  7.88 us (4%)
  local copies, waits for them, and re-layouts  6.28 us (3%)
    all_gather x1, waiting for transfers between devices, on_device(): big = lax.all_gather(wide, 'col', axis=0, tiled=True)  40.3 us
    ppermute x20, waiting for transfers between devices, shifted(): return lax.ppermute(x, axis, pairs)  35.2 us
    ppermute x20, starting transfers between devices, shifted(): return lax.ppermute(x, axis, pairs)  22.5 us
    all_to_all x3, starting transfers between devices, exchange(): return lax.all_to_all(x, axis, split_axis=0, concat_axis=0, tiled=True)  21.6 us
    all_to_all x3, waiting for transfers between devices, exchange(): return lax.all_to_all(x, axis, split_axis=0, concat_axis=0, tiled=True)  16.7 us
    pallas_call x1, Pallas kernels, attn_call(): pl.pallas_call(attn_kernel, grid=(1,), in_specs=[smem, smem, smem, whole(...  7 us
    pallas_call x1, Pallas kernels, decode_call(): pl.pallas_call(decode_kernel, grid=(1,), in_specs=[smem if i in (0, 9, 10...  5.24 us
    pallas_call x1, Pallas kernels, early_call(): pl.pallas_call(early_kernel, grid=(3,), in_specs=[pl.BlockSpec(memory_spa...  4.14 us
  transfers between devices with their start and end apart: 24, of which 22 were waited for; matrix products, arithmetic and copies ran while one was open for 6% of the time, Pallas kernels for 11%

profile of v3, /device:TPU:38, one launch (start us, length us, event | category | flops | bytes accessed | tf_op | source)
XLA Modules:
  0.0 190.0 jit_solution(7459701626088286746)
XLA Ops:
  7.2 2.0 %pack.1 = (bf16[32,40,128]{2,1,0:T(8,128)(2,1)}, bf16[32,1920]{1,0:T(8,128)(2,1)}) custom-call(s32[8,16]{1,0:T(8,128)} %bitcast.111, s32[16]{0:T(128)} %len_ref.1, s32[16]{0:T(128)} %var_ref.1, s32[1,16]{1,0:T(1,128)} %bitcast.109, bf16[528,128]{1,0:T(8,128)(2,1)} %x_ref.1, bf16[32,128]{1,0:T(8,128)(2,1)} %w_ref.1, bf16[32,512]{1,0:T(8,128)(2,1)} %refs_0_.1, ...), custom_call_target="tpu_custom_call" | custom-call | bytes 1048576 | tf_op jit(solution)/shard_map/pack/pallas_call | solution.py:94
  9.2 11.4 %all-to-all-start = ((bf16[32,40,128]{2,1,0:T(8,128)(2,1)}), bf16[32,40,128]{2,1,0:T(8,128)(2,1)S(1)}, u32[]{:S(2)}, u32[]{:S(2)}) async-start(bf16[32,40,128]{2,1,0:T(8,128)(2,1)} %get-tuple-element.21), calls=%async_computation | async-start | bytes 655360 | tf_op jit(solution)/shard_map/all_to_all | solution.py:501
  21.5 1.9 fusion
  23.3 10.7 %all-to-all-done.w_ref.wq_ref = bf16[32,40,128]{2,1,0:T(8,128)(2,1)S(1)} async-done(((bf16[32,40,128]{2,1,0:T(8,128)(2,1)}), bf16[32,40,128]{2,1,0:T(8,128)(2,1)S(1)}, u32[]{:S(2)}, u32[]{:S(2)}) %all-to-all-start) | async-done | bytes 327712 | tf_op jit(solution)/shard_map/all_to_all | solution.py:501
  34.6 2.4 %collective-permute-start.5 = (bf16[64,128]{1,0:T(8,128)(2,1)S(1)}, bf16[64,128]{1,0:T(8,128)(2,1)S(1)}, u32[]{:S(2)}, u32[]{:S(2)}) collective-permute-start(bf16[64,128]{1,0:T(8,128)(2,1)S(1)} %bitcast.97), channel_id=1, source_target_pairs={{0,128},{32,160},{64,192},{96,224},{128,0},{160,32},{192,64},{224,... | collective-permute-start | bytes 49160 | tf_op jit(solution)/shard_map/ppermute | solution.py:482
  39.9 2.2 %collective-permute-done.6 = bf16[64,128]{1,0:T(8,128)(2,1)S(1)} collective-permute-done((bf16[64,128]{1,0:T(8,128)(2,1)S(1)}, bf16[64,128]{1,0:T(8,128)(2,1)S(1)}, u32[]{:S(2)}, u32[]{:S(2)}) %collective-permute-start.6) | collective-permute-done | bytes 16416 | tf_op jit(solution)/shard_map/ppermute | solution.py:482
  44.0 5.2 %decode.1 = bf16[32,8,128]{2,1,0:T(8,128)(2,1)} custom-call(s32[2]{0:T(128)} %pad_add_fusion.me_ref, bf16[4,64,128]{2,1,0:T(8,128)(2,1)} %copy-done.10, bf16[4,64,128]{2,1,0:T(8,128)(2,1)} %copy-done.11, f32[1,1024]{1,0:T(1,128)} %bitcast.103, bf16[32,40,128]{2,1,0:T(8,128)(2,1)} %copy-done.4, f32[64,128]{1,0:T(8,128)} %get-tuple-element.54.cos_ref, ...), custom_call_target="tpu_custom_call" | custom-call | flops 268435456 | bytes 3145728 | tf_op jit(solution)/shard_map/decode/pallas_call | solution.py:364
  49.3 4.6 %all-to-all-start.1 = ((bf16[32,8,128]{2,1,0:T(8,128)(2,1)}), bf16[32,8,128]{2,1,0:T(8,128)(2,1)S(1)}, u32[]{:S(2)}, u32[]{:S(2)}) async-start(bf16[32,8,128]{2,1,0:T(8,128)(2,1)} %decode.1), calls=%async_computation.1 | async-start | bytes 131072 | tf_op jit(solution)/shard_map/all_to_all | solution.py:501
  54.0 3.1 %gather_fusion = bf16[64,2,128,128]{3,2,1,0:T(8,128)(2,1)} fusion(bf16[32,2,128,128]{3,2,1,0:T(8,128)(2,1)S(1)} %copy-done.3, s32[1024]{0:T(1024)S(1)} %pad_clamp_fusion), kind=kCustom, calls=%fused_computation | custom fusion | bytes 8388864 | tf_op jit(solution)/shard_map/gather | solution.py:565
  57.0 6.0 %all-to-all-done.1 = bf16[32,8,128]{2,1,0:T(8,128)(2,1)S(1)} async-done(((bf16[32,8,128]{2,1,0:T(8,128)(2,1)}), bf16[32,8,128]{2,1,0:T(8,128)(2,1)S(1)}, u32[]{:S(2)}, u32[]{:S(2)}) %all-to-all-start.1) | async-done | bytes 65568 | tf_op jit(solution)/shard_map/all_to_all | solution.py:501
  63.6 5.6 %all-to-all-start.2 = ((bf16[32,2,2,128,128]{4,3,2,1,0:T(8,128)(2,1)}), bf16[32,2,2,128,128]{4,3,2,1,0:T(8,128)(2,1)}, u32[]{:S(2)}, u32[]{:S(2)}) async-start(bf16[32,2,2,128,128]{4,3,2,1,0:T(8,128)(2,1)} %bitcast.85), calls=%async_computation.2 | async-start | bytes 8388608 | tf_op jit(solution)/shard_map/all_to_all | solution.py:501
  72.2 2.5 %collective-permute-done = bf16[528,128]{1,0:T(8,128)(2,1)S(1)} collective-permute-done((bf16[528,128]{1,0:T(8,128)(2,1)S(1)}, bf16[528,128]{1,0:T(8,128)(2,1)S(1)}, u32[]{:S(2)}, u32[]{:S(2)}) %collective-permute-start) | collective-permute-done | bytes 135200 | tf_op jit(solution)/shard_map/ppermute | solution.py:482
  74.7 2.2 %collective-permute-done.1 = bf16[528,128]{1,0:T(8,128)(2,1)S(1)} collective-permute-done((bf16[528,128]{1,0:T(8,128)(2,1)S(1)}, bf16[528,128]{1,0:T(8,128)(2,1)S(1)}, u32[]{:S(2)}, u32[]{:S(2)}) %collective-permute-start.1) | collective-permute-done | bytes 135200 | tf_op jit(solution)/shard_map/ppermute | solution.py:482
  81.3 4.1 %early.1 = (bf16[528,1024]{1,0:T(8,128)(2,1)}, bf16[528,128]{1,0:T(8,128)(2,1)}) custom-call(s32[2]{0:T(128)} %pad_add_fusion.me_ref, bf16[4,528,128]{2,1,0:T(8,128)(2,1)} %copy-done.5, bf16[4,528,128]{2,1,0:T(8,128)(2,1)} %copy-done.8, f32[1,1024]{1,0:T(1,128)} %bitcast.104, bf16[32,40,128]{2,1,0:T(8,128)(2,1)} %copy-done.4, ...), custom_call_target="tpu_custom_call" | custom-call | flops 138412032 | bytes 4194304 | tf_op jit(solution)/shard_map/early/pallas_call | solution.py:129
  85.4 40.3 %all-gather.2.cloned.1.call-done.wk_ref.wv_ref.wo_ref.gate_ref.up_ref.down_ref = bf16[1024,1920]{1,0:T(8,128)(2,1)} async-done(((bf16[32,1920]{1,0:T(8,128)(2,1)}), bf16[1024,1920]{1,0:T(8,128)(2,1)}) %all-gather.2.cloned.1.call-update) | async-done | bytes 3932176 | tf_op jit(solution)/shard_map/all_gather | solution.py:552
  125.7 7.0 %attn.1 = (bf16[16,256]{1,0:T(8,128)(2,1)}, bf16[4,2,128,128]{3,2,1,0:T(8,128)(2,1)}, bf16[4,528,128]{2,1,0:T(8,128)(2,1)}, bf16[4,528,128]{2,1,0:T(8,128)(2,1)}) custom-call(s32[2]{0:T(128)} %pad_add_fusion.me_ref, f32[2]{0:T(128)} %bsame_ref.3, f32[2]{0:T(128)} %bdiff_ref.3, bf16[528,1024]{1,0:T(8,128)(2,1)} %get-tuple-element.24.normed_ref, ...), custom_call_target="tpu_custom_call" | custom-call | flops 683671552 | bytes 6291456 | tf_op jit(solution)/shard_map/attn/pallas_call | solution.py:260
  132.7 2.1 %collective-permute-done.8 = bf16[4,528,128]{2,1,0:T(8,128)(2,1)S(1)} collective-permute-done((bf16[4,528,128]{2,1,0:T(8,128)(2,1)}, bf16[4,528,128]{2,1,0:T(8,128)(2,1)S(1)}, u32[]{:S(2)}, u32[]{:S(2)}) %collective-permute-start.8) | collective-permute-done | bytes 540704 | tf_op jit(solution)/shard_map/ppermute | solution.py:482
  136.2 5.1 %collective-permute-start.10 = (bf16[528,128]{1,0:T(8,128)(2,1)S(1)}, bf16[528,128]{1,0:T(8,128)(2,1)S(1)}, u32[]{:S(2)}, u32[]{:S(2)}) collective-permute-start(bf16[528,128]{1,0:T(8,128)(2,1)S(1)} %get-tuple-element.48), channel_id=1, source_target_pairs={{0,128},{32,160},{64,192},{96,224},{128,0},{160,32},{192,64},{224,... | collective-permute-start | bytes 405512 | tf_op jit(solution)/shard_map/ppermute | solution.py:482
  141.4 3.1 %collective-permute-start.9 = (bf16[528,128]{1,0:T(8,128)(2,1)S(1)}, bf16[528,128]{1,0:T(8,128)(2,1)S(1)}, u32[]{:S(2)}, u32[]{:S(2)}) collective-permute-start(bf16[528,128]{1,0:T(8,128)(2,1)S(1)} %get-tuple-element.46), channel_id=1, source_target_pairs={{0,64},{32,96},{64,128},{96,160},{128,192},{160,224},{192,0},{224,... | collective-permute-start | bytes 405512 | tf_op jit(solution)/shard_map/ppermute | solution.py:482
  145.3 2.8 %collective-permute-done.11 = bf16[528,128]{1,0:T(8,128)(2,1)S(1)} collective-permute-done((bf16[528,128]{1,0:T(8,128)(2,1)S(1)}, bf16[528,128]{1,0:T(8,128)(2,1)S(1)}, u32[]{:S(2)}, u32[]{:S(2)}) %collective-permute-start.11) | collective-permute-done | bytes 135200 | tf_op jit(solution)/shard_map/ppermute | solution.py:482
  148.2 3.0 %collective-permute-start.12 = (bf16[528,128]{1,0:T(8,128)(2,1)S(1)}, bf16[528,128]{1,0:T(8,128)(2,1)S(1)}, u32[]{:S(2)}, u32[]{:S(2)}) collective-permute-start(bf16[528,128]{1,0:T(8,128)(2,1)S(1)} %fusion.26), channel_id=1, source_target_pairs={{0,64},{32,96},{64,128},{96,160},{128,192},{160,224},{192,0},{224,... | collective-permute-start | bytes 405512 | tf_op jit(solution)/shard_map/ppermute | solution.py:482
  151.2 2.4 %collective-permute-start.13 = (bf16[528,128]{1,0:T(8,128)(2,1)S(1)}, bf16[528,128]{1,0:T(8,128)(2,1)S(1)}, u32[]{:S(2)}, u32[]{:S(2)}) collective-permute-start(bf16[528,128]{1,0:T(8,128)(2,1)S(1)} %fusion.26), channel_id=1, source_target_pairs={{0,128},{32,160},{64,192},{96,224},{128,0},{160,32},{192,64},{224,... | collective-permute-start | bytes 405512 | tf_op jit(solution)/shard_map/ppermute | solution.py:482
  153.6 2.3 %collective-permute-done.12 = bf16[528,128]{1,0:T(8,128)(2,1)S(1)} collective-permute-done((bf16[528,128]{1,0:T(8,128)(2,1)S(1)}, bf16[528,128]{1,0:T(8,128)(2,1)S(1)}, u32[]{:S(2)}, u32[]{:S(2)}) %collective-permute-start.12) | collective-permute-done | bytes 135200 | tf_op jit(solution)/shard_map/ppermute | solution.py:482
  155.9 3.3 %collective-permute-done.13 = bf16[528,128]{1,0:T(8,128)(2,1)S(1)} collective-permute-done((bf16[528,128]{1,0:T(8,128)(2,1)S(1)}, bf16[528,128]{1,0:T(8,128)(2,1)S(1)}, u32[]{:S(2)}, u32[]{:S(2)}) %collective-permute-start.13) | collective-permute-done | bytes 135200 | tf_op jit(solution)/shard_map/ppermute | solution.py:482
  159.2 1.8 collective-permute-done.14
  161.2 1.9 %collective-permute-done.15.rb_ref = bf16[4,528,128]{2,1,0:T(8,128)(2,1)S(1)} collective-permute-done((bf16[4,528,128]{2,1,0:T(8,128)(2,1)S(1)}, bf16[4,528,128]{2,1,0:T(8,128)(2,1)S(1)}, u32[]{:S(2)}, u32[]{:S(2)}) %collective-permute-start.15) | collective-permute-done | bytes 540704 | tf_op jit(solution)/shard_map/ppermute | solution.py:482
  163.1 4.0 %ffn.1 = (bf16[4,528,128]{2,1,0:T(8,128)(2,1)S(1)}, bf16[4,528,128]{2,1,0:T(8,128)(2,1)S(1)}) custom-call(s32[2]{0:T(128)S(1)} %copy-done.1, bf16[4,528,128]{2,1,0:T(8,128)(2,1)S(1)} %pad_maximum_fusion.1.ra_ref, bf16[4,528,128]{2,1,0:T(8,128)(2,1)S(1)} %collective-permute-done.15.rb_ref, f32[1,1024]{1,0:T(1,128)S(1)} %bitcast.84, ...), custom_call_target="tpu_custom_call" | custom-call | flops 1660944384 | bytes 6291456 | tf_op jit(solution)/shard_map/ffn/pallas_call | solution.py:401
  167.3 1.8 collective-permute-done.16
  169.5 2.8 %collective-permute-start.18 = (bf16[528,128]{1,0:T(8,128)(2,1)S(1)}, bf16[528,128]{1,0:T(8,128)(2,1)S(1)}, u32[]{:S(2)}, u32[]{:S(2)}) collective-permute-start(bf16[528,128]{1,0:T(8,128)(2,1)S(1)} %get-tuple-element.45), channel_id=1, source_target_pairs={{0,128},{32,160},{64,192},{96,224},{128,0},{160,32},{192,64},{224,... | collective-permute-start | bytes 405512 | tf_op jit(solution)/shard_map/ppermute | solution.py:482
  172.9 2.9 %collective-permute-done.17 = bf16[528,128]{1,0:T(8,128)(2,1)S(1)} collective-permute-done((bf16[528,128]{1,0:T(8,128)(2,1)S(1)}, bf16[528,128]{1,0:T(8,128)(2,1)S(1)}, u32[]{:S(2)}, u32[]{:S(2)}) %collective-permute-start.17) | collective-permute-done | bytes 135200 | tf_op jit(solution)/shard_map/ppermute | solution.py:482
  177.4 2.1 %collective-permute-done.19 = bf16[528,128]{1,0:T(8,128)(2,1)S(1)} collective-permute-done((bf16[528,128]{1,0:T(8,128)(2,1)S(1)}, bf16[528,128]{1,0:T(8,128)(2,1)S(1)}, u32[]{:S(2)}, u32[]{:S(2)}) %collective-permute-start.19) | collective-permute-done | bytes 135200 | tf_op jit(solution)/shard_map/ppermute | solution.py:482
  180.3 2.9 %tail.1 = bf16[16,2,128,128]{3,2,1,0:T(8,128)(2,1)} custom-call(s32[16]{0:T(128)} %get-tuple-element.35.target_ref, s32[16]{0:T(128)} %get-tuple-element.36.row_ref, bf16[16,256]{1,0:T(8,128)(2,1)} %get-tuple-element.37.new_ref, bf16[64,2,128,128]{3,2,1,0:T(8,128)(2,1)} %bitcast.43.pages_ref), custom_call_target="tpu_custom_call" | custom-call | bytes 4194304 | tf_op jit(solution)/shard_map/tail/pallas_call | solution.py:452
  (83 shorter events, 20.4 us)
Async XLA Ops:
  7.2 14.3 %copy-start.14 = (s32[16]{0:T(128)S(1)}, s32[16]{0:T(128)}, u32[]{:S(2)}) copy-start(s32[16]{0:T(128)} %len_ref.1) | copy-start | bytes 196
  7.2 13.5 %copy-start.12 = (s32[1,512]{1,0:T(1,128)S(1)}, s32[1,512]{1,0:T(1,128)}, u32[]{:S(2)}) copy-start(s32[1,512]{1,0:T(1,128)} %vrow_ref.1) | copy-start | bytes 6148
  7.2 118.5 %all-gather.2.cloned.1.call-start = ((), (), s32[]{:S(2)}) async-start(), calls=%async_computation.3 | async-start | bytes 4055040 | tf_op jit(solution)/shard_map/all_gather | solution.py:552
  9.2 24.8 %all-to-all-start = ((bf16[32,40,128]{2,1,0:T(8,128)(2,1)}), bf16[32,40,128]{2,1,0:T(8,128)(2,1)S(1)}, u32[]{:S(2)}, u32[]{:S(2)}) async-start(bf16[32,40,128]{2,1,0:T(8,128)(2,1)} %get-tuple-element.21), calls=%async_computation | async-start | bytes 655360 | tf_op jit(solution)/shard_map/all_to_all | solution.py:501
  34.0 9.4 %copy-start.4 = (bf16[32,40,128]{2,1,0:T(8,128)(2,1)}, bf16[32,40,128]{2,1,0:T(8,128)(2,1)S(1)}, u32[]{:S(2)}) copy-start(bf16[32,40,128]{2,1,0:T(8,128)(2,1)S(1)} %all-to-all-done.w_ref.wq_ref) | copy-start | bytes 983044
  34.1 4.3 %collective-permute-start.4 = (bf16[64,128]{1,0:T(8,128)(2,1)S(1)}, bf16[64,128]{1,0:T(8,128)(2,1)S(1)}, u32[]{:S(2)}, u32[]{:S(2)}) collective-permute-start(bf16[64,128]{1,0:T(8,128)(2,1)S(1)} %bitcast.96), channel_id=1, source_target_pairs={{0,64},{32,96},{64,128},{96,160},{128,192},{160,224},{192,0},{224,... | collective-permute-start | bytes 49160 | tf_op jit(solution)/shard_map/ppermute | solution.py:482
  34.6 5.2 %collective-permute-start.5 = (bf16[64,128]{1,0:T(8,128)(2,1)S(1)}, bf16[64,128]{1,0:T(8,128)(2,1)S(1)}, u32[]{:S(2)}, u32[]{:S(2)}) collective-permute-start(bf16[64,128]{1,0:T(8,128)(2,1)S(1)} %bitcast.97), channel_id=1, source_target_pairs={{0,128},{32,160},{64,192},{96,224},{128,0},{160,32},{192,64},{224,... | collective-permute-start | bytes 49160 | tf_op jit(solution)/shard_map/ppermute | solution.py:482
  37.1 4.9 %collective-permute-start.6 = (bf16[64,128]{1,0:T(8,128)(2,1)S(1)}, bf16[64,128]{1,0:T(8,128)(2,1)S(1)}, u32[]{:S(2)}, u32[]{:S(2)}) collective-permute-start(bf16[64,128]{1,0:T(8,128)(2,1)S(1)} %bitcast.98), channel_id=1, source_target_pairs={{0,192},{32,224},{64,0},{96,32},{128,64},{160,96},{192,128},{224,1... | collective-permute-start | bytes 49160 | tf_op jit(solution)/shard_map/ppermute | solution.py:482
  42.1 1.3 collective-permute-start.7
  44.0 9.9 %copy-start.3 = (bf16[32,2,128,128]{3,2,1,0:T(8,128)(2,1)S(1)}, bf16[32,2,128,128]{3,2,1,0:T(8,128)(2,1)}, u32[]{:S(2)}) copy-start(bf16[32,2,128,128]{3,2,1,0:T(8,128)(2,1)} %pool_ref.1) | copy-start | bytes 6291460
  49.3 13.7 %all-to-all-start.1 = ((bf16[32,8,128]{2,1,0:T(8,128)(2,1)}), bf16[32,8,128]{2,1,0:T(8,128)(2,1)S(1)}, u32[]{:S(2)}, u32[]{:S(2)}) async-start(bf16[32,8,128]{2,1,0:T(8,128)(2,1)} %decode.1), calls=%async_computation.1 | async-start | bytes 131072 | tf_op jit(solution)/shard_map/all_to_all | solution.py:501
  63.6 116.7 %all-to-all-start.2 = ((bf16[32,2,2,128,128]{4,3,2,1,0:T(8,128)(2,1)}), bf16[32,2,2,128,128]{4,3,2,1,0:T(8,128)(2,1)}, u32[]{:S(2)}, u32[]{:S(2)}) async-start(bf16[32,2,2,128,128]{4,3,2,1,0:T(8,128)(2,1)} %bitcast.85), calls=%async_computation.2 | async-start | bytes 8388608 | tf_op jit(solution)/shard_map/all_to_all | solution.py:501
  69.2 9.3 %copy-start.13 = (s32[16,1]{0,1:T(1,128)S(1)}, s32[16,1]{0,1:T(1,128)}, u32[]{:S(2)}) copy-start(s32[16,1]{0,1:T(1,128)} %param.41) | copy-start | bytes 196
  69.2 5.5 %collective-permute-start = (bf16[528,128]{1,0:T(8,128)(2,1)S(1)}, bf16[528,128]{1,0:T(8,128)(2,1)S(1)}, u32[]{:S(2)}, u32[]{:S(2)}) collective-permute-start(bf16[528,128]{1,0:T(8,128)(2,1)S(1)} %copy-done.6), channel_id=1, source_target_pairs={{0,64},{32,96},{64,128},{96,160},{128,192},{160,224},{192,0},{224,... | collective-permute-start | bytes 405512 | tf_op jit(solution)/shard_map/ppermute | solution.py:482
  69.9 7.0 %collective-permute-start.1 = (bf16[528,128]{1,0:T(8,128)(2,1)S(1)}, bf16[528,128]{1,0:T(8,128)(2,1)S(1)}, u32[]{:S(2)}, u32[]{:S(2)}) collective-permute-start(bf16[528,128]{1,0:T(8,128)(2,1)S(1)} %copy-done.6), channel_id=1, source_target_pairs={{0,128},{32,160},{64,192},{96,224},{128,0},{160,32},{192,64},{224,... | collective-permute-start | bytes 405512 | tf_op jit(solution)/shard_map/ppermute | solution.py:482
  70.8 7.4 %collective-permute-start.2 = (bf16[528,128]{1,0:T(8,128)(2,1)S(1)}, bf16[528,128]{1,0:T(8,128)(2,1)S(1)}, u32[]{:S(2)}, u32[]{:S(2)}) collective-permute-start(bf16[528,128]{1,0:T(8,128)(2,1)S(1)} %copy-done.6), channel_id=1, source_target_pairs={{0,192},{32,224},{64,0},{96,32},{128,64},{160,96},{192,128},{224,1... | collective-permute-start | bytes 405512 | tf_op jit(solution)/shard_map/ppermute | solution.py:482
  78.3 2.2 %collective-permute-start.3 = (bf16[4,528,128]{2,1,0:T(8,128)(2,1)S(1)}, bf16[4,528,128]{2,1,0:T(8,128)(2,1)S(1)}, u32[]{:S(2)}, u32[]{:S(2)}) collective-permute-start(bf16[4,528,128]{2,1,0:T(8,128)(2,1)S(1)} %pad_maximum_fusion.xa_ref), channel_id=1, source_target_pairs={{0,32},{32,0},{64,96},{96,64},{128,160},{160,128},{192,224},{224,1... | collective-permute-start | bytes 1622024 | tf_op jit(solution)/shard_map/ppermute | solution.py:482
  132.7 2.1 %collective-permute-start.8 = (bf16[4,528,128]{2,1,0:T(8,128)(2,1)}, bf16[4,528,128]{2,1,0:T(8,128)(2,1)S(1)}, u32[]{:S(2)}, u32[]{:S(2)}) collective-permute-start(bf16[4,528,128]{2,1,0:T(8,128)(2,1)} %get-tuple-element.29), channel_id=1, source_target_pairs={{0,32},{32,0},{64,96},{96,64},{128,160},{160,128},{192,224},{224,1... | collective-permute-start | bytes 1622024 | tf_op jit(solution)/shard_map/ppermute | solution.py:482
  134.8 28.3 %copy-start = (bf16[1024,1920]{1,0:T(8,128)(2,1)S(1)}, bf16[1024,1920]{1,0:T(8,128)(2,1)}, u32[]{:S(2)}) copy-start(bf16[1024,1920]{1,0:T(8,128)(2,1)} %all-gather.2.cloned.1.call-done.wk_ref.wv_ref.wo_ref.gate_ref.up_ref.down_ref) | copy-start | bytes 11796484
  136.2 26.9 %copy-start.1 = (s32[2]{0:T(128)S(1)}, s32[2]{0:T(128)}, u32[]{:S(2)}) copy-start(s32[2]{0:T(128)} %pad_add_fusion.me_ref) | copy-start | bytes 28
  136.2 26.9 %copy-start.2 = (f32[1024]{0:T(1024)S(1)}, f32[1024]{0:T(1024)}, u32[]{:S(2)}) copy-start(f32[1024]{0:T(1024)} %param.31) | copy-start | bytes 12292
  136.2 9.1 %collective-permute-start.10 = (bf16[528,128]{1,0:T(8,128)(2,1)S(1)}, bf16[528,128]{1,0:T(8,128)(2,1)S(1)}, u32[]{:S(2)}, u32[]{:S(2)}) collective-permute-start(bf16[528,128]{1,0:T(8,128)(2,1)S(1)} %get-tuple-element.48), channel_id=1, source_target_pairs={{0,128},{32,160},{64,192},{96,224},{128,0},{160,32},{192,64},{224,... | collective-permute-start | bytes 405512 | tf_op jit(solution)/shard_map/ppermute | solution.py:482
  141.3 6.8 %collective-permute-start.11 = (bf16[528,128]{1,0:T(8,128)(2,1)S(1)}, bf16[528,128]{1,0:T(8,128)(2,1)S(1)}, u32[]{:S(2)}, u32[]{:S(2)}) collective-permute-start(bf16[528,128]{1,0:T(8,128)(2,1)S(1)} %get-tuple-element.47), channel_id=1, source_target_pairs={{0,192},{32,224},{64,0},{96,32},{128,64},{160,96},{192,128},{224,1... | collective-permute-start | bytes 405512 | tf_op jit(solution)/shard_map/ppermute | solution.py:482
  141.4 6.7 %collective-permute-start.9 = (bf16[528,128]{1,0:T(8,128)(2,1)S(1)}, bf16[528,128]{1,0:T(8,128)(2,1)S(1)}, u32[]{:S(2)}, u32[]{:S(2)}) collective-permute-start(bf16[528,128]{1,0:T(8,128)(2,1)S(1)} %get-tuple-element.46), channel_id=1, source_target_pairs={{0,64},{32,96},{64,128},{96,160},{128,192},{160,224},{192,0},{224,... | collective-permute-start | bytes 405512 | tf_op jit(solution)/shard_map/ppermute | solution.py:482
  148.2 7.7 %collective-permute-start.12 = (bf16[528,128]{1,0:T(8,128)(2,1)S(1)}, bf16[528,128]{1,0:T(8,128)(2,1)S(1)}, u32[]{:S(2)}, u32[]{:S(2)}) collective-permute-start(bf16[528,128]{1,0:T(8,128)(2,1)S(1)} %fusion.26), channel_id=1, source_target_pairs={{0,64},{32,96},{64,128},{96,160},{128,192},{160,224},{192,0},{224,... | collective-permute-start | bytes 405512 | tf_op jit(solution)/shard_map/ppermute | solution.py:482
  151.2 8.0 %collective-permute-start.13 = (bf16[528,128]{1,0:T(8,128)(2,1)S(1)}, bf16[528,128]{1,0:T(8,128)(2,1)S(1)}, u32[]{:S(2)}, u32[]{:S(2)}) collective-permute-start(bf16[528,128]{1,0:T(8,128)(2,1)S(1)} %fusion.26), channel_id=1, source_target_pairs={{0,128},{32,160},{64,192},{96,224},{128,0},{160,32},{192,64},{224,... | collective-permute-start | bytes 405512 | tf_op jit(solution)/shard_map/ppermute | solution.py:482
  153.6 7.4 %collective-permute-start.14 = (bf16[528,128]{1,0:T(8,128)(2,1)S(1)}, bf16[528,128]{1,0:T(8,128)(2,1)S(1)}, u32[]{:S(2)}, u32[]{:S(2)}) collective-permute-start(bf16[528,128]{1,0:T(8,128)(2,1)S(1)} %fusion.26), channel_id=1, source_target_pairs={{0,192},{32,224},{64,0},{96,32},{128,64},{160,96},{192,128},{224,1... | collective-permute-start | bytes 405512 | tf_op jit(solution)/shard_map/ppermute | solution.py:482
  161.1 2.0 %collective-permute-start.15 = (bf16[4,528,128]{2,1,0:T(8,128)(2,1)S(1)}, bf16[4,528,128]{2,1,0:T(8,128)(2,1)S(1)}, u32[]{:S(2)}, u32[]{:S(2)}) collective-permute-start(bf16[4,528,128]{2,1,0:T(8,128)(2,1)S(1)} %pad_maximum_fusion.1.ra_ref), channel_id=1, source_target_pairs={{0,32},{32,0},{64,96},{96,64},{128,160},{160,128},{192,224},{224,1... | collective-permute-start | bytes 1622024 | tf_op jit(solution)/shard_map/ppermute | solution.py:482
  167.1 2.0 %collective-permute-start.16 = (bf16[4,528,128]{2,1,0:T(8,128)(2,1)S(1)}, bf16[4,528,128]{2,1,0:T(8,128)(2,1)S(1)}, u32[]{:S(2)}, u32[]{:S(2)}) collective-permute-start(bf16[4,528,128]{2,1,0:T(8,128)(2,1)S(1)} %get-tuple-element.31), channel_id=1, source_target_pairs={{0,32},{32,0},{64,96},{96,64},{128,160},{160,128},{192,224},{224,1... | collective-permute-start | bytes 1622024 | tf_op jit(solution)/shard_map/ppermute | solution.py:482
  169.3 6.5 %collective-permute-start.17 = (bf16[528,128]{1,0:T(8,128)(2,1)S(1)}, bf16[528,128]{1,0:T(8,128)(2,1)S(1)}, u32[]{:S(2)}, u32[]{:S(2)}) collective-permute-start(bf16[528,128]{1,0:T(8,128)(2,1)S(1)} %get-tuple-element.43), channel_id=1, source_target_pairs={{0,64},{32,96},{64,128},{96,160},{128,192},{160,224},{192,0},{224,... | collective-permute-start | bytes 405512 | tf_op jit(solution)/shard_map/ppermute | solution.py:482
  169.5 7.9 %collective-permute-start.18 = (bf16[528,128]{1,0:T(8,128)(2,1)S(1)}, bf16[528,128]{1,0:T(8,128)(2,1)S(1)}, u32[]{:S(2)}, u32[]{:S(2)}) collective-permute-start(bf16[528,128]{1,0:T(8,128)(2,1)S(1)} %get-tuple-element.45), channel_id=1, source_target_pairs={{0,128},{32,160},{64,192},{96,224},{128,0},{160,32},{192,64},{224,... | collective-permute-start | bytes 405512 | tf_op jit(solution)/shard_map/ppermute | solution.py:482
  172.3 7.2 %collective-permute-start.19 = (bf16[528,128]{1,0:T(8,128)(2,1)S(1)}, bf16[528,128]{1,0:T(8,128)(2,1)S(1)}, u32[]{:S(2)}, u32[]{:S(2)}) collective-permute-start(bf16[528,128]{1,0:T(8,128)(2,1)S(1)} %get-tuple-element.44), channel_id=1, source_target_pairs={{0,192},{32,224},{64,0},{96,32},{128,64},{160,96},{192,128},{224,1... | collective-permute-start | bytes 405512 | tf_op jit(solution)/shard_map/ppermute | solution.py:482
  (7 other events, 18.1 us)
Sparse Core Ops, SparseCore 0:
  11.2 114.4 all-gather.1
